TPU v7x, 512 devices: a whole 4x8x8 slice. The times are simulated.
512 devices in a mesh: row: 64 (over y_hi, x, z), col: 8 (over y_lo, core).
Axes of the slice: x: 4, y: 8 (y_hi: 2, y_lo: 4; y = y_hi * 4 + y_lo), z: 8, core: 2. Of those that a mesh axis runs over, the one named last changes fastest.
Arguments:
- features: bfloat16 [65536, 1024], P(('row', 'col')), may hold values from -6 to 6
- history: bfloat16 [65536, 1024], P(('row', 'col')), may hold values from -6 to 6
- degree: int32 [65536], P(('row', 'col')), may hold values from 8 to 64
- adj_tiles: bfloat16 [3072, 128, 128], P(('row', 'col')), may hold values from 0 to 3, as said below
- tile_index: int32 [3072], P(('row', 'col')), may hold values from 0 to 23, as said below
- tile_count: int32 [512], P(('row', 'col')), may hold values from 3 to 6, as said below
- weight: bfloat16 [1024, 1024], P(None, 'col'), may hold values from -0.1875 to 0.1875
- cotangent: bfloat16 [65536, 1024], P(('row', 'col')), may hold values from -6 to 6
Outputs:
- layer_out: bfloat16 [65536, 1024], P(('row', 'col'))
- grad_features: bfloat16 [65536, 1024], P(('row', 'col'))
- grad_weight: float32 [1024, 1024], P(None, 'col')
Inputs may be any that keep to these rules, and one draw needn't show every extreme that they name: `adj_tiles`: whole numbers: the edge counts of a tile's entries. Slots from tile_count on of a device are never read. `tile_index`: the codes of one device's 6 slots are distinct. Its first three slots hold tiles whose column block lies in the first, the last and the middle third of the 3 m column blocks, in that order. `tile_count`: some device has 6 live slots in every draw.
All inputs are finite; a program needn't handle non-finite values.
Results may differ from a plain program's by a relative error of at most 0.014.
Values may be sent and summed in bfloat16 or wider, within the bound.
No kernel may reach another device: no remote copies, remote signals or barrier semaphores. Data moves between devices by JAX's collectives and lax.ppermute only.
A program may use at most 64 MiB of HBM per device.

v0:
```python
import math

import jax
import jax.numpy as jnp
from jax import lax
from jax.experimental import pallas as pl
from jax.experimental.pallas import tpu as pltpu
from jax.sharding import PartitionSpec as P

TILE = 128
CORES = 2
RING = 8
PAD = 16
GRANT = 12 << 20
F32 = jnp.float32
BF16 = jnp.bfloat16


def paired(x, axis, start):
    pairs = [(i, i + 1) for i in range(start, lax.axis_size(axis) - 1, 2)]
    return lax.ppermute(x, axis, pairs + [(j, i) for i, j in pairs])


def swap(x):
    return lax.ppermute(x, "col", [(i, i ^ 1) for i in range(lax.axis_size("col"))])


def rotate(x, by):
    cols = lax.axis_size("col")
    chips = cols // CORES
    pairs = [(i, (i // CORES + by) % chips * CORES + i % CORES) for i in range(cols)]
    return lax.ppermute(x, "col", pairs)


def gather(x):
    chips = lax.axis_size("col") // CORES
    same = [x] + [rotate(x, by) for by in range(1, chips)]
    return same + [swap(block) for block in same]


def origins(me, chips):
    chip, core = me // CORES, me % CORES
    same = [(chip - by + chips) % chips * CORES + core for by in range(chips)]
    return same + [at + 1 - 2 * core for at in same]


def vmem(count):
    return [pl.BlockSpec(memory_space=pltpu.VMEM)] * count


def smem(count):
    return [pl.BlockSpec(memory_space=pltpu.SMEM)] * count


def call(kernel, outs, ins, scratch=(), flops=0, transcendentals=0):
    specs = vmem(len(outs))
    return pl.pallas_call(
        kernel,
        out_shape=tuple(jax.ShapeDtypeStruct(shape, kind) for shape, kind in outs),
        in_specs=smem(ins[0]) + vmem(ins[1]),
        out_specs=tuple(specs),
        scratch_shapes=list(scratch),
        compiler_params=pltpu.CompilerParams(vmem_limit_bytes=GRANT),
        cost_estimate=pl.CostEstimate(
            flops=flops, bytes_accessed=2 << 20, transcendentals=transcendentals
        ),
    )


def pack_kernel(where, cot, weight, degree, out):
    count, _, cols = out.shape
    slab = cot.shape[0]
    depth = out.shape[1] - slab - PAD
    part = weight[pl.ds(pl.multiple_of(where[1] * depth, depth), depth), :]
    row = jnp.broadcast_to(degree[...].astype(F32).astype(BF16), (PAD, cols))
    for at in range(count):
        out[at, :slab, :] = cot[:, at * cols : (at + 1) * cols]
        out[at, slab : slab + depth, :] = part
        out[at, slab + depth :, :] = row


def prepare_kernel(where, index, count, tiles, feats, scale, block, middle, own):
    slots, slab = tiles.shape[0], feats.shape[0]
    width = 3 * slab // TILE
    part_rows = block.shape[0]
    chips = part_rows // slab // CORES
    chip, core = where[0] // CORES, where[0] % CORES
    block[...] = jnp.zeros_like(block)
    middle[...] = jnp.zeros_like(middle)
    for slot in range(slots):

        @pl.when(slot < count[0])
        def _():
            code = index[slot]
            dest, src = code // width, code % width
            other = (dest % CORES + core) % CORES * chips
            ahead = (dest // CORES - chip + chips) % chips
            row = pl.multiple_of((other + ahead) * TILE, TILE)
            odd = where[1] % 2
            col = pl.multiple_of((src + 2 * odd * (1 - src)) * TILE, TILE)
            block[pl.ds(row, TILE), pl.ds(col, TILE)] = tiles[slot]

            @pl.when(src == 1)
            def _():
                middle[pl.ds(pl.multiple_of(dest * TILE, TILE), TILE), :] = tiles[slot]

    own[...] = (feats[...].astype(F32) * scale[...]).astype(BF16)


def aggregate_kernel(block, first, own, second, mine, theirs):
    slab = own.shape[0]
    half = mine.shape[0]
    step = 256
    for out, base in ((theirs, half), (mine, 0)):
        for at in range(0, half, step):
            here = slice(base + at, base + at + step)
            total = jnp.dot(block[here, :slab], first[...], preferred_element_type=F32)
            total += jnp.dot(block[here, slab : 2 * slab], own[...], preferred_element_type=F32)
            total += jnp.dot(block[here, 2 * slab :], second[...], preferred_element_type=F32)
            out[at : at + step, :] = total.astype(BF16)


def main_kernel(where, packed, weight, *refs):
    *aggs, grads, parts = refs
    slab, width = aggs[0].shape
    pieces = parts.shape[0]
    rows = lax.broadcasted_iota(jnp.int32, (slab, slab), 0)
    eye = rows == lax.broadcasted_iota(jnp.int32, (slab, slab), 1)
    total = None
    for at, agg in zip(origins(where[0], len(aggs) // CORES), aggs):
        degree = packed[at, packed.shape[1] - PAD :, :][:1, :].astype(F32)
        scale = jnp.sum(jnp.where(eye, 1.0 / jnp.sqrt(degree), 0.0), axis=1, keepdims=True)
        pre = jnp.dot(agg[...], weight[...], preferred_element_type=F32) * scale
        sig = jax.nn.sigmoid(pre)
        slope = sig * (1.0 + pre * (1.0 - sig))
        grad = (packed[at, :slab, :].astype(F32) * slope * scale).astype(BF16)
        grads[pl.ds(pl.multiple_of(at * slab, slab), slab), :] = grad
        part = lax.dot_general(
            grad, agg[...], (((0,), (0,)), ((), ())), preferred_element_type=F32
        )
        total = part if total is None else total + part
    total = total.astype(BF16)
    for at in range(pieces):
        parts[at] = total[:, at * (width // pieces) : (at + 1) * (width // pieces)]


def final_kernel(where, weight, other, agg, middle, scale, *refs):
    *same, others, layer_out, out, mixed, whole = refs
    outer, chips, depth, cols = weight.shape
    for blocks, core in ((weight, where[0] % CORES), (other, 1 - where[0] % CORES)):
        for chip in range(chips):
            here = pl.ds(pl.multiple_of((chip * CORES + core) * cols, cols), cols)
            for step in range(outer):
                whole[step * depth : (step + 1) * depth, here] = blocks[step, chip]
    step = 256
    for at in range(0, out.shape[1], step):
        here = slice(at, at + step)
        pre = jnp.dot(agg[...], whole[:, here], preferred_element_type=F32) * scale[...]
        layer_out[:, here] = (pre * jax.nn.sigmoid(pre)).astype(BF16)
    grads = [*same, *[others.at[at] for at in range(chips)]]
    for at, grad in zip(origins(where[0], chips), grads):
        part = lax.dot_general(
            middle[...], grad[...], (((0,), (0,)), ((), ())), preferred_element_type=F32
        )
        mixed[:, pl.ds(pl.multiple_of(at * cols, cols), cols)] = part.astype(BF16)
    for at in range(0, out.shape[1], step):
        here = slice(at, at + step)
        back = lax.dot_general(
            mixed[...], whole[here, :], (((1,), (1,)), ((), ())), preferred_element_type=F32
        )
        out[:, here] = (back * scale[...]).astype(BF16)


def per_device(features, history, degree, adj_tiles, tile_index, tile_count, weight, cotangent):
    slab, width = features.shape
    cols, rows = lax.axis_size("col"), lax.axis_size("row")
    chips = cols // CORES
    part_rows = slab * cols
    out_cols = width // cols
    depth = width // RING
    outer = rows // RING
    near = [[RING * i + j for j in range(RING)] for i in range(outer)]
    half = rows // 2
    across = [
        [half * i + RING * k + j for k in range(outer // 2)] for i in range(2) for j in range(RING)
    ]
    where = jnp.stack([lax.axis_index("col"), lax.axis_index("row") % RING]).astype(jnp.int32)

    def total(x):
        return jnp.sum(x.astype(F32), axis=0)

    def over_row(x, groups):
        return lax.all_to_all(x, "row", 0, 0, tiled=True, axis_index_groups=groups)

    def replicated(x, groups):
        count = len(groups[0])
        return over_row(jnp.broadcast_to(x[None], (count, *x.shape)), groups)

    scale = (1.0 / jnp.sqrt(degree.astype(F32)))[:, None]
    hist_src = (history.astype(F32) * scale).astype(BF16)
    first = paired(hist_src, "row", 1)
    second = paired(hist_src, "row", 0)
    packed = call(
        pack_kernel, [((cols, slab + depth + PAD, out_cols), BF16)], (1, 3)
    )(where, cotangent, weight, degree[None])[0]
    packed = lax.all_to_all(packed, "col", 0, 0, tiled=True)
    block, middle, own = call(
        prepare_kernel,
        [((part_rows, 3 * slab), BF16), ((part_rows, slab), BF16), ((slab, width), BF16)],
        (3, 3),
    )(where, tile_index, tile_count, adj_tiles, features, scale)
    mine, theirs = call(
        aggregate_kernel,
        [((part_rows // CORES, width), BF16)] * 2,
        (0, 4),
        flops=6 * part_rows * slab * width,
    )(block, first, own, second)
    other = swap(theirs)
    arrived = []
    for by in range(1, chips):
        here = slice(by * slab, (by + 1) * slab)
        ahead = (mine[here].astype(F32) + other[here].astype(F32)).astype(BF16)
        arrived.append(rotate(ahead, by))
    agg = mine[:slab].astype(F32) + other[:slab].astype(F32)
    agg = (agg + sum(block.astype(F32) for block in arrived)).astype(BF16)
    core = where[0] % CORES
    mine_cols = packed.reshape(chips, CORES, slab + depth + PAD, out_cols)
    mine_cols = lax.dynamic_index_in_dim(mine_cols, core, 1, keepdims=False)
    half_weight = replicated(mine_cols[:, slab : slab + depth, :], near)
    other_weight = swap(half_weight)
    aggs = gather(agg)
    grad, parts = call(
        main_kernel,
        [((part_rows, out_cols), BF16), ((RING, out_cols, depth), BF16)],
        (1, 2 + cols),
        flops=4 * part_rows * width * out_cols,
        transcendentals=part_rows * out_cols,
    )(where, packed, weight, *aggs)
    summed = over_row(parts, near)
    grads = [grad] + [rotate(grad, by) for by in range(1, chips)]
    others = swap(jnp.stack(grads))
    summed = total(summed).T.astype(BF16)
    summed = replicated(summed, across)
    summed = total(summed).astype(BF16)
    opposite = lax.ppermute(summed, "row", [(i, (i + half) % rows) for i in range(rows)])
    summed = summed.astype(F32) + opposite.astype(F32)
    summed = summed * (1.0 / math.sqrt(part_rows * rows))
    summed = replicated(summed.astype(BF16), near)
    grad_weight = summed.reshape(width, out_cols).astype(F32)
    layer_out, grad_features = call(
        final_kernel,
        [((slab, width), BF16)] * 2,
        (1, 6 + chips),
        [pltpu.VMEM((slab, width), BF16), pltpu.VMEM((width, width), BF16)],
        flops=6 * slab * width * width,
        transcendentals=slab * width,
    )(where, half_weight, other_weight, agg, middle, scale, *grads, others)
    return layer_out, grad_features, grad_weight


def solution(mesh):
    both = ("row", "col")
    in_specs = (
        P(both, None),
        P(both, None),
        P(both),
        P(both, None, None),
        P(both),
        P(both),
        P(None, "col"),
        P(both, None),
    )
    out_specs = (P(both, None), P(both, None), P(None, "col"))
    return jax.shard_map(
        per_device, mesh=mesh, in_specs=in_specs, out_specs=out_specs, check_vma=False
    )
```

profile of v0, /device:TPU:26, one launch (start us, length us, event | category | flops | bytes accessed | tf_op | source)
XLA Modules:
  0.0 206.1 jit_solution(8454008637922362589)
XLA Ops:
  0.6 0.7 convert_rsqrt_fusion
  1.3 1.1 multiply_convert_fusion
  2.4 10.9 %collective-permute-start.1 = (bf16[128,1024]{1,0:T(8,128)(2,1)S(1)}, bf16[128,1024]{1,0:T(8,128)(2,1)S(1)}, u32[]{:S(2)}, u32[]{:S(2)}) collective-permute-start(bf16[128,1024]{1,0:T(8,128)(2,1)S(1)} %multiply_convert_fusion), channel_id=1, source_target_pairs={{8,16},{24,32},{40,48},{56,64},{72,80},{88,96},{104,112},{120,128}... | collective-permute-start | bytes 786440 | tf_op jit(solution)/shard_map/ppermute | solution.py:21
  13.3 1.9 collective-permute-start.2
  15.3 0.1 copy.16.scale
  16.1 0.1 pad_add_fusion.where
  16.2 0.6 copy-done.16
  16.7 0.9 shard_map.104
  17.7 0.7 copy-done.10
  18.4 1.3 collective-permute-done.1.first
  19.6 0.7 copy-done.17
  20.3 2.7 %collective-permute-done.2.second = bf16[128,1024]{1,0:T(8,128)(2,1)S(1)} collective-permute-done((bf16[128,1024]{1,0:T(8,128)(2,1)S(1)}, bf16[128,1024]{1,0:T(8,128)(2,1)S(1)}, u32[]{:S(2)}, u32[]{:S(2)}) %collective-permute-start.2) | collective-permute-done | bytes 262176 | tf_op jit(solution)/shard_map/ppermute | solution.py:21
  23.0 0.7 copy-done.19
  23.7 0.9 copy-done.18
  24.7 0.9 copy-done.20
  25.6 1.8 shard_map.105
  27.4 1.9 collective-permute-start.3
  29.3 2.6 %collective-permute-done.3 = bf16[512,1024]{1,0:T(8,128)(2,1)S(1)} collective-permute-done((bf16[512,1024]{1,0:T(8,128)(2,1)S(1)}, bf16[512,1024]{1,0:T(8,128)(2,1)S(1)}, u32[]{:S(2)}, u32[]{:S(2)}) %collective-permute-start.3) | collective-permute-done | bytes 1048608 | tf_op jit(solution)/shard_map/ppermute | solution.py:25
  31.9 0.3 add_convert_fusion.3
  32.3 0.7 copy-done.21
  32.9 2.1 %collective-permute-start.4 = (bf16[128,1024]{1,0:T(8,128)(2,1)S(1)}, bf16[128,1024]{1,0:T(8,128)(2,1)S(1)}, u32[]{:S(2)}, u32[]{:S(2)}) collective-permute-start(bf16[128,1024]{1,0:T(8,128)(2,1)S(1)} %get-tuple-element.21), channel_id=1, source_target_pairs={{0,2},{1,3},{2,4},{3,5},{4,6},{5,7},{6,0},{7,1},{8,10},{9,11},{10,... | collective-permute-start | bytes 786440 | tf_op jit(solution)/shard_map/ppermute | solution.py:32
  35.1 3.6 %collective-permute-start.5 = (bf16[128,1024]{1,0:T(8,128)(2,1)S(1)}, bf16[128,1024]{1,0:T(8,128)(2,1)}, u32[]{:S(2)}, u32[]{:S(2)}) collective-permute-start(bf16[128,1024]{1,0:T(8,128)(2,1)S(1)} %get-tuple-element.23), channel_id=1, source_target_pairs={{0,4},{1,5},{2,6},{3,7},{4,0},{5,1},{6,2},{7,3},{8,12},{9,13},{10,... | collective-permute-start | bytes 786440 | tf_op jit(solution)/shard_map/ppermute | solution.py:32
  38.7 2.4 %collective-permute-start.6 = (bf16[128,1024]{1,0:T(8,128)(2,1)S(1)}, bf16[128,1024]{1,0:T(8,128)(2,1)}, u32[]{:S(2)}, u32[]{:S(2)}) collective-permute-start(bf16[128,1024]{1,0:T(8,128)(2,1)S(1)} %get-tuple-element.22), channel_id=1, source_target_pairs={{0,6},{1,7},{2,0},{3,1},{4,2},{5,3},{6,4},{7,5},{8,14},{9,15},{10,... | collective-permute-start | bytes 786440 | tf_op jit(solution)/shard_map/ppermute | solution.py:32
  41.1 1.5 shard_map.103
  42.5 6.8 %all-to-all-start = ((bf16[8,272,128]{2,1,0:T(8,128)(2,1)}), bf16[8,272,128]{2,1,0:T(8,128)(2,1)S(1)}, u32[]{:S(2)}, u32[]{:S(2)}) async-start(bf16[8,272,128]{2,1,0:T(8,128)(2,1)} %shard_map.103), calls=%async_computation | async-start | bytes 1114112 | tf_op jit(solution)/shard_map/all_to_all | solution.py:206
  49.4 17.5 %collective-permute-done.5 = bf16[128,1024]{1,0:T(8,128)(2,1)} collective-permute-done((bf16[128,1024]{1,0:T(8,128)(2,1)S(1)}, bf16[128,1024]{1,0:T(8,128)(2,1)}, u32[]{:S(2)}, u32[]{:S(2)}) %collective-permute-start.5) | collective-permute-done | bytes 262176 | tf_op jit(solution)/shard_map/ppermute | solution.py:32
  66.9 1.3 add_convert_fusion.refs_0_.agg
  68.2 1.9 collective-permute-start.7
  70.1 2.5 %collective-permute-start.8 = (bf16[128,1024]{1,0:T(8,128)(2,1)S(1)}, bf16[128,1024]{1,0:T(8,128)(2,1)S(1)}, u32[]{:S(2)}, u32[]{:S(2)}) collective-permute-start(bf16[128,1024]{1,0:T(8,128)(2,1)S(1)} %add_convert_fusion.refs_0_.agg), channel_id=1, source_target_pairs={{0,4},{1,5},{2,6},{3,7},{4,0},{5,1},{6,2},{7,3},{8,12},{9,13},{10,... | collective-permute-start | bytes 786440 | tf_op jit(solution)/shard_map/ppermute | solution.py:32
  72.6 3.9 %collective-permute-start.9 = (bf16[128,1024]{1,0:T(8,128)(2,1)S(1)}, bf16[128,1024]{1,0:T(8,128)(2,1)S(1)}, u32[]{:S(2)}, u32[]{:S(2)}) collective-permute-start(bf16[128,1024]{1,0:T(8,128)(2,1)S(1)} %add_convert_fusion.refs_0_.agg), channel_id=1, source_target_pairs={{0,6},{1,7},{2,0},{3,1},{4,2},{5,3},{6,4},{7,5},{8,14},{9,15},{10,... | collective-permute-start | bytes 786440 | tf_op jit(solution)/shard_map/ppermute | solution.py:32
  76.5 1.9 collective-permute-start.10
  78.5 2.4 %collective-permute-start.11 = (bf16[128,1024]{1,0:T(8,128)(2,1)S(1)}, bf16[128,1024]{1,0:T(8,128)(2,1)S(1)}, u32[]{:S(2)}, u32[]{:S(2)}) collective-permute-start(bf16[128,1024]{1,0:T(8,128)(2,1)S(1)} %collective-permute-done.7.refs_1_), channel_id=1, source_target_pairs={{0,1},{1,0},{2,3},{3,2},{4,5},{5,4},{6,7},{7,6},{8,9},{9,8},{10,11... | collective-permute-start | bytes 786440 | tf_op jit(solution)/shard_map/ppermute | solution.py:25
  80.9 13.5 %collective-permute-done.8.refs_2_ = bf16[128,1024]{1,0:T(8,128)(2,1)S(1)} collective-permute-done((bf16[128,1024]{1,0:T(8,128)(2,1)S(1)}, bf16[128,1024]{1,0:T(8,128)(2,1)S(1)}, u32[]{:S(2)}, u32[]{:S(2)}) %collective-permute-start.8) | collective-permute-done | bytes 262176 | tf_op jit(solution)/shard_map/ppermute | solution.py:32
  94.4 1.9 collective-permute-start.12
  96.3 2.4 %collective-permute-start.13 = (bf16[128,1024]{1,0:T(8,128)(2,1)S(1)}, bf16[128,1024]{1,0:T(8,128)(2,1)S(1)}, u32[]{:S(2)}, u32[]{:S(2)}) collective-permute-start(bf16[128,1024]{1,0:T(8,128)(2,1)S(1)} %collective-permute-done.9.refs_3_), channel_id=1, source_target_pairs={{0,1},{1,0},{2,3},{3,2},{4,5},{5,4},{6,7},{7,6},{8,9},{9,8},{10,11... | collective-permute-start | bytes 786440 | tf_op jit(solution)/shard_map/ppermute | solution.py:25
  98.7 1.1 collective-permute-done.13.refs_7_
  99.8 3.1 %shard_map.106 = (bf16[1024,128]{1,0:T(8,128)(2,1)S(1)}, bf16[8,128,128]{2,1,0:T(8,128)(2,1)S(1)}) custom-call(s32[2]{0:T(128)S(1)} %pad_add_fusion.where, bf16[8,272,128]{2,1,0:T(8,128)(2,1)S(1)} %all-to-all-done.packed, bf16[1024,128]{1,0:T(8,128)(2,1)S(1)} %copy-done, bf16[128,1024]{1,0:T(8,128)(2,1)S(1)} %add_convert_fusion.refs_0_.agg, ...), custom_call_target="tpu_custom_call" | custom-call | flops 536870912 | bytes 2097152 | tf_op jit(solution)/shard_map/pallas_call | solution.py:232
  103.0 0.7 copy-done.13
  103.6 3.4 %all-to-all-start.2 = ((bf16[8,128,128]{2,1,0:T(8,128)(2,1)}), bf16[8,128,128]{2,1,0:T(8,128)(2,1)S(1)}, u32[]{:S(2)}, u32[]{:S(2)}) async-start(bf16[8,128,128]{2,1,0:T(8,128)(2,1)} %copy-done.13), calls=%async_computation.2 | async-start | bytes 524288 | tf_op jit(solution)/shard_map/all_to_all | solution.py:193
  107.1 12.5 %all-to-all-done.2 = bf16[8,128,128]{2,1,0:T(8,128)(2,1)S(1)} async-done(((bf16[8,128,128]{2,1,0:T(8,128)(2,1)}), bf16[8,128,128]{2,1,0:T(8,128)(2,1)S(1)}, u32[]{:S(2)}, u32[]{:S(2)}) %all-to-all-start.2) | async-done | bytes 262176 | tf_op jit(solution)/shard_map/all_to_all | solution.py:193
  119.7 1.2 broadcast_in_dim.11
  120.9 3.6 %all-to-all-start.1 = ((bf16[8,4,128,128]{3,2,1,0:T(8,128)(2,1)}), bf16[8,4,128,128]{3,2,1,0:T(8,128)(2,1)S(1)}, u32[]{:S(2)}, u32[]{:S(2)}) async-start(bf16[8,4,128,128]{3,2,1,0:T(8,128)(2,1)} %broadcast_in_dim.11), calls=%async_computation.1 | async-start | bytes 2097152 | tf_op jit(solution)/shard_map/all_to_all | solution.py:193
  124.5 1.9 collective-permute-start.14
  126.4 1.9 collective-permute-start.15
  128.3 3.9 %collective-permute-start.16 = (bf16[1024,128]{1,0:T(8,128)(2,1)S(1)}, bf16[1024,128]{1,0:T(8,128)(2,1)S(1)}, u32[]{:S(2)}, u32[]{:S(2)}) collective-permute-start(bf16[1024,128]{1,0:T(8,128)(2,1)S(1)} %get-tuple-element.17.refs_0_), channel_id=1, source_target_pairs={{0,6},{1,7},{2,0},{3,1},{4,2},{5,3},{6,4},{7,5},{8,14},{9,15},{10,... | collective-permute-start | bytes 786440 | tf_op jit(solution)/shard_map/ppermute | solution.py:32
  132.3 0.1 copy.18
  132.4 21.2 %all-to-all-done.1.weight = bf16[8,4,128,128]{3,2,1,0:T(8,128)(2,1)S(1)} async-done(((bf16[8,4,128,128]{3,2,1,0:T(8,128)(2,1)}), bf16[8,4,128,128]{3,2,1,0:T(8,128)(2,1)S(1)}, u32[]{:S(2)}, u32[]{:S(2)}) %all-to-all-start.1) | async-done | bytes 1048608 | tf_op jit(solution)/shard_map/all_to_all | solution.py:193
  153.7 0.7 broadcast_in_dim.13
  154.3 14.8 %all-to-all-start.3 = ((bf16[4,128,128]{2,1,0:T(8,128)(2,1)}), bf16[4,128,128]{2,1,0:T(8,128)(2,1)}, u32[]{:S(2)}, u32[]{:S(2)}) async-start(bf16[4,128,128]{2,1,0:T(8,128)(2,1)} %broadcast_in_dim.13), calls=%async_computation.3 | async-start | bytes 262144 | tf_op jit(solution)/shard_map/all_to_all | solution.py:193
  169.2 1.1 pad_maximum_fusion
  170.3 0.7 copy-done.3
  171.0 0.7 copy-done.5
  171.7 0.7 copy-done.7
  172.5 1.9 collective-permute-start.17
  174.4 2.4 %collective-permute-start = (bf16[8,4,128,128]{3,2,1,0:T(8,128)(2,1)S(1)}, bf16[8,4,128,128]{3,2,1,0:T(8,128)(2,1)S(1)}, u32[]{:S(2)}, u32[]{:S(2)}) collective-permute-start(bf16[8,4,128,128]{3,2,1,0:T(8,128)(2,1)S(1)} %all-to-all-done.1.weight), channel_id=1, source_target_pairs={{0,1},{1,0},{2,3},{3,2},{4,5},{5,4},{6,7},{7,6},{8,9},{9,8},{10,11... | collective-permute-start | bytes 3145736 | tf_op jit(solution)/shard_map/ppermute | solution.py:25
  176.8 0.9 reduce_sum.25
  177.7 1.9 collective-permute-start.18
  179.7 7.8 %collective-permute-done.18 = bf16[128,128]{1,0:T(8,128)(2,1)S(1)} collective-permute-done((bf16[128,128]{1,0:T(8,128)(2,1)S(1)}, bf16[128,128]{1,0:T(8,128)(2,1)S(1)}, u32[]{:S(2)}, u32[]{:S(2)}) %collective-permute-start.18) | collective-permute-done | bytes 32800 | tf_op jit(solution)/shard_map/ppermute | solution.py:245
  187.5 13.7 %all_to_all.25 = bf16[8,128,128]{2,1,0:T(8,128)(2,1)S(1)} all-to-all(bf16[8,128,128]{2,1,0:T(8,128)(2,1)S(1)} %broadcast_in_dim.28), channel_id=1, replica_groups={{0,8,16,24,32,40,48,56},{64,72,80,88,96,104,112,120},{128,136,144,152,1..., dimensions={0} | all-to-all | bytes 524288 | tf_op jit(solution)/shard_map/all_to_all | solution.py:193
  201.3 0.8 bitcast_convert_fusion
  202.1 0.1 copy-done.2
  202.2 0.3 copy-done.4
  202.5 0.1 copy-done.6
  202.5 3.6 %shard_map.107 = (bf16[128,1024]{1,0:T(8,128)(2,1)}, bf16[128,1024]{1,0:T(8,128)(2,1)}) custom-call(s32[2]{0:T(128)S(1)} %pad_add_fusion.where, bf16[8,4,128,128]{3,2,1,0:T(8,128)(2,1)S(1)} %all-to-all-done.1.weight, bf16[8,4,128,128]{3,2,1,0:T(8,128)(2,1)S(1)} %collective-permute-done.other, bf16[128,1024]{1,0:T(8,128)(2,1)S(1)} %add_convert_fusion.refs_0_.agg, ...), custom_call_target="tpu_custom_call" | custom-call | flops 805306368 | bytes 2097152 | tf_op jit(solution)/shard_map/pallas_call | solution.py:250
  (49 shorter events, 0.2 us)
Async XLA Ops:
  1.3 14.9 %copy-start.12 = (bf16[128,1024]{1,0:T(8,128)(2,1)S(1)}, bf16[128,1024]{1,0:T(8,128)(2,1)}, u32[]{:S(2)}) copy-start(bf16[128,1024]{1,0:T(8,128)(2,1)} %feats.1) | copy-start | bytes 786436
  1.3 14.9 %copy-start.14 = (bf16[6,128,128]{2,1,0:T(8,128)(2,1)S(1)}, bf16[6,128,128]{2,1,0:T(8,128)(2,1)}, u32[]{:S(2)}) copy-start(bf16[6,128,128]{2,1,0:T(8,128)(2,1)} %tiles.1) | copy-start | bytes 589828
  2.4 17.2 %collective-permute-start.1 = (bf16[128,1024]{1,0:T(8,128)(2,1)S(1)}, bf16[128,1024]{1,0:T(8,128)(2,1)S(1)}, u32[]{:S(2)}, u32[]{:S(2)}) collective-permute-start(bf16[128,1024]{1,0:T(8,128)(2,1)S(1)} %multiply_convert_fusion), channel_id=1, source_target_pairs={{8,16},{24,32},{40,48},{56,64},{72,80},{88,96},{104,112},{120,128}... | collective-permute-start | bytes 786440 | tf_op jit(solution)/shard_map/ppermute | solution.py:21
  13.3 9.7 %collective-permute-start.2 = (bf16[128,1024]{1,0:T(8,128)(2,1)S(1)}, bf16[128,1024]{1,0:T(8,128)(2,1)S(1)}, u32[]{:S(2)}, u32[]{:S(2)}) collective-permute-start(bf16[128,1024]{1,0:T(8,128)(2,1)S(1)} %multiply_convert_fusion), channel_id=1, source_target_pairs={{0,8},{16,24},{32,40},{48,56},{64,72},{80,88},{96,104},{112,120},{... | collective-permute-start | bytes 786440 | tf_op jit(solution)/shard_map/ppermute | solution.py:21
  16.1 0.7 copy-start.16
  17.7 0.7 copy-start.10
  19.6 0.7 copy-start.17
  23.0 0.7 copy-start.19
  23.7 0.9 copy-start.18
  24.7 0.9 copy-start.20
  27.4 4.6 %collective-permute-start.3 = (bf16[512,1024]{1,0:T(8,128)(2,1)S(1)}, bf16[512,1024]{1,0:T(8,128)(2,1)S(1)}, u32[]{:S(2)}, u32[]{:S(2)}) collective-permute-start(bf16[512,1024]{1,0:T(8,128)(2,1)S(1)} %get-tuple-element.15), channel_id=1, source_target_pairs={{0,1},{1,0},{2,3},{3,2},{4,5},{5,4},{6,7},{7,6},{8,9},{9,8},{10,11... | collective-permute-start | bytes 3145736 | tf_op jit(solution)/shard_map/ppermute | solution.py:25
  31.9 1.0 copy-start.21
  31.9 9.1 %copy-start = (bf16[1024,128]{1,0:T(8,128)(2,1)S(1)}, bf16[1024,128]{1,0:T(8,128)(2,1)}, u32[]{:S(2)}) copy-start(bf16[1024,128]{1,0:T(8,128)(2,1)} %weight.3) | copy-start | bytes 786436
  31.9 9.1 %copy-start.9 = (bf16[128,1024]{1,0:T(8,128)(2,1)S(1)}, bf16[128,1024]{1,0:T(8,128)(2,1)}, u32[]{:S(2)}) copy-start(bf16[128,1024]{1,0:T(8,128)(2,1)} %cot.1) | copy-start | bytes 786436
  32.9 16.4 %collective-permute-start.4 = (bf16[128,1024]{1,0:T(8,128)(2,1)S(1)}, bf16[128,1024]{1,0:T(8,128)(2,1)S(1)}, u32[]{:S(2)}, u32[]{:S(2)}) collective-permute-start(bf16[128,1024]{1,0:T(8,128)(2,1)S(1)} %get-tuple-element.21), channel_id=1, source_target_pairs={{0,2},{1,3},{2,4},{3,5},{4,6},{5,7},{6,0},{7,1},{8,10},{9,11},{10,... | collective-permute-start | bytes 786440 | tf_op jit(solution)/shard_map/ppermute | solution.py:32
  35.1 31.8 %collective-permute-start.5 = (bf16[128,1024]{1,0:T(8,128)(2,1)S(1)}, bf16[128,1024]{1,0:T(8,128)(2,1)}, u32[]{:S(2)}, u32[]{:S(2)}) collective-permute-start(bf16[128,1024]{1,0:T(8,128)(2,1)S(1)} %get-tuple-element.23), channel_id=1, source_target_pairs={{0,4},{1,5},{2,6},{3,7},{4,0},{5,1},{6,2},{7,3},{8,12},{9,13},{10,... | collective-permute-start | bytes 786440 | tf_op jit(solution)/shard_map/ppermute | solution.py:32
  38.7 2.4 %copy-start.15 = (s32[128]{0:T(128)S(1)}, s32[128]{0:T(128)}, u32[]{:S(2)}) copy-start(s32[128]{0:T(128)} %param.10) | copy-start | bytes 1540
  38.7 28.2 %collective-permute-start.6 = (bf16[128,1024]{1,0:T(8,128)(2,1)S(1)}, bf16[128,1024]{1,0:T(8,128)(2,1)}, u32[]{:S(2)}, u32[]{:S(2)}) collective-permute-start(bf16[128,1024]{1,0:T(8,128)(2,1)S(1)} %get-tuple-element.22), channel_id=1, source_target_pairs={{0,6},{1,7},{2,0},{3,1},{4,2},{5,3},{6,4},{7,5},{8,14},{9,15},{10,... | collective-permute-start | bytes 786440 | tf_op jit(solution)/shard_map/ppermute | solution.py:32
  42.5 56.2 %all-to-all-start = ((bf16[8,272,128]{2,1,0:T(8,128)(2,1)}), bf16[8,272,128]{2,1,0:T(8,128)(2,1)S(1)}, u32[]{:S(2)}, u32[]{:S(2)}) async-start(bf16[8,272,128]{2,1,0:T(8,128)(2,1)} %shard_map.103), calls=%async_computation | async-start | bytes 1114112 | tf_op jit(solution)/shard_map/all_to_all | solution.py:206
  68.2 10.3 %collective-permute-start.7 = (bf16[128,1024]{1,0:T(8,128)(2,1)S(1)}, bf16[128,1024]{1,0:T(8,128)(2,1)S(1)}, u32[]{:S(2)}, u32[]{:S(2)}) collective-permute-start(bf16[128,1024]{1,0:T(8,128)(2,1)S(1)} %add_convert_fusion.refs_0_.agg), channel_id=1, source_target_pairs={{0,2},{1,3},{2,4},{3,5},{4,6},{5,7},{6,0},{7,1},{8,10},{9,11},{10,... | collective-permute-start | bytes 786440 | tf_op jit(solution)/shard_map/ppermute | solution.py:32
  70.1 24.2 %collective-permute-start.8 = (bf16[128,1024]{1,0:T(8,128)(2,1)S(1)}, bf16[128,1024]{1,0:T(8,128)(2,1)S(1)}, u32[]{:S(2)}, u32[]{:S(2)}) collective-permute-start(bf16[128,1024]{1,0:T(8,128)(2,1)S(1)} %add_convert_fusion.refs_0_.agg), channel_id=1, source_target_pairs={{0,4},{1,5},{2,6},{3,7},{4,0},{5,1},{6,2},{7,3},{8,12},{9,13},{10,... | collective-permute-start | bytes 786440 | tf_op jit(solution)/shard_map/ppermute | solution.py:32
  72.6 23.7 %collective-permute-start.9 = (bf16[128,1024]{1,0:T(8,128)(2,1)S(1)}, bf16[128,1024]{1,0:T(8,128)(2,1)S(1)}, u32[]{:S(2)}, u32[]{:S(2)}) collective-permute-start(bf16[128,1024]{1,0:T(8,128)(2,1)S(1)} %add_convert_fusion.refs_0_.agg), channel_id=1, source_target_pairs={{0,6},{1,7},{2,0},{3,1},{4,2},{5,3},{6,4},{7,5},{8,14},{9,15},{10,... | collective-permute-start | bytes 786440 | tf_op jit(solution)/shard_map/ppermute | solution.py:32
  76.5 22.2 %collective-permute-start.10 = (bf16[128,1024]{1,0:T(8,128)(2,1)S(1)}, bf16[128,1024]{1,0:T(8,128)(2,1)S(1)}, u32[]{:S(2)}, u32[]{:S(2)}) collective-permute-start(bf16[128,1024]{1,0:T(8,128)(2,1)S(1)} %add_convert_fusion.refs_0_.agg), channel_id=1, source_target_pairs={{0,1},{1,0},{2,3},{3,2},{4,5},{5,4},{6,7},{7,6},{8,9},{9,8},{10,11... | collective-permute-start | bytes 786440 | tf_op jit(solution)/shard_map/ppermute | solution.py:25
  78.5 20.2 %collective-permute-start.11 = (bf16[128,1024]{1,0:T(8,128)(2,1)S(1)}, bf16[128,1024]{1,0:T(8,128)(2,1)S(1)}, u32[]{:S(2)}, u32[]{:S(2)}) collective-permute-start(bf16[128,1024]{1,0:T(8,128)(2,1)S(1)} %collective-permute-done.7.refs_1_), channel_id=1, source_target_pairs={{0,1},{1,0},{2,3},{3,2},{4,5},{5,4},{6,7},{7,6},{8,9},{9,8},{10,11... | collective-permute-start | bytes 786440 | tf_op jit(solution)/shard_map/ppermute | solution.py:25
  94.4 4.4 %collective-permute-start.12 = (bf16[128,1024]{1,0:T(8,128)(2,1)S(1)}, bf16[128,1024]{1,0:T(8,128)(2,1)S(1)}, u32[]{:S(2)}, u32[]{:S(2)}) collective-permute-start(bf16[128,1024]{1,0:T(8,128)(2,1)S(1)} %collective-permute-done.8.refs_2_), channel_id=1, source_target_pairs={{0,1},{1,0},{2,3},{3,2},{4,5},{5,4},{6,7},{7,6},{8,9},{9,8},{10,11... | collective-permute-start | bytes 786440 | tf_op jit(solution)/shard_map/ppermute | solution.py:25
  96.3 3.6 %collective-permute-start.13 = (bf16[128,1024]{1,0:T(8,128)(2,1)S(1)}, bf16[128,1024]{1,0:T(8,128)(2,1)S(1)}, u32[]{:S(2)}, u32[]{:S(2)}) collective-permute-start(bf16[128,1024]{1,0:T(8,128)(2,1)S(1)} %collective-permute-done.9.refs_3_), channel_id=1, source_target_pairs={{0,1},{1,0},{2,3},{3,2},{4,5},{5,4},{6,7},{7,6},{8,9},{9,8},{10,11... | collective-permute-start | bytes 786440 | tf_op jit(solution)/shard_map/ppermute | solution.py:25
  102.9 0.7 copy-start.13
  103.6 65.5 %copy-start.1 = (bf16[1024,128]{1,0:T(8,128)(2,1)}, bf16[1024,128]{1,0:T(8,128)(2,1)S(1)}, u32[]{:S(2)}) copy-start(bf16[1024,128]{1,0:T(8,128)(2,1)S(1)} %get-tuple-element.17.refs_0_) | copy-start | bytes 786436
  103.6 16.0 %all-to-all-start.2 = ((bf16[8,128,128]{2,1,0:T(8,128)(2,1)}), bf16[8,128,128]{2,1,0:T(8,128)(2,1)S(1)}, u32[]{:S(2)}, u32[]{:S(2)}) async-start(bf16[8,128,128]{2,1,0:T(8,128)(2,1)} %copy-done.13), calls=%async_computation.2 | async-start | bytes 524288 | tf_op jit(solution)/shard_map/all_to_all | solution.py:193
  120.9 32.8 %all-to-all-start.1 = ((bf16[8,4,128,128]{3,2,1,0:T(8,128)(2,1)}), bf16[8,4,128,128]{3,2,1,0:T(8,128)(2,1)S(1)}, u32[]{:S(2)}, u32[]{:S(2)}) async-start(bf16[8,4,128,128]{3,2,1,0:T(8,128)(2,1)} %broadcast_in_dim.11), calls=%async_computation.1 | async-start | bytes 2097152 | tf_op jit(solution)/shard_map/all_to_all | solution.py:193
  124.5 44.7 %collective-permute-start.14 = (bf16[1024,128]{1,0:T(8,128)(2,1)S(1)}, bf16[1024,128]{1,0:T(8,128)(2,1)S(1)}, u32[]{:S(2)}, u32[]{:S(2)}) collective-permute-start(bf16[1024,128]{1,0:T(8,128)(2,1)S(1)} %get-tuple-element.17.refs_0_), channel_id=1, source_target_pairs={{0,2},{1,3},{2,4},{3,5},{4,6},{5,7},{6,0},{7,1},{8,10},{9,11},{10,... | collective-permute-start | bytes 786440 | tf_op jit(solution)/shard_map/ppermute | solution.py:32
  126.4 42.8 %collective-permute-start.15 = (bf16[1024,128]{1,0:T(8,128)(2,1)S(1)}, bf16[1024,128]{1,0:T(8,128)(2,1)S(1)}, u32[]{:S(2)}, u32[]{:S(2)}) collective-permute-start(bf16[1024,128]{1,0:T(8,128)(2,1)S(1)} %get-tuple-element.17.refs_0_), channel_id=1, source_target_pairs={{0,4},{1,5},{2,6},{3,7},{4,0},{5,1},{6,2},{7,3},{8,12},{9,13},{10,... | collective-permute-start | bytes 786440 | tf_op jit(solution)/shard_map/ppermute | solution.py:32
  128.3 40.8 %collective-permute-start.16 = (bf16[1024,128]{1,0:T(8,128)(2,1)S(1)}, bf16[1024,128]{1,0:T(8,128)(2,1)S(1)}, u32[]{:S(2)}, u32[]{:S(2)}) collective-permute-start(bf16[1024,128]{1,0:T(8,128)(2,1)S(1)} %get-tuple-element.17.refs_0_), channel_id=1, source_target_pairs={{0,6},{1,7},{2,0},{3,1},{4,2},{5,3},{6,4},{7,5},{8,14},{9,15},{10,... | collective-permute-start | bytes 786440 | tf_op jit(solution)/shard_map/ppermute | solution.py:32
  154.3 22.5 %all-to-all-start.3 = ((bf16[4,128,128]{2,1,0:T(8,128)(2,1)}), bf16[4,128,128]{2,1,0:T(8,128)(2,1)}, u32[]{:S(2)}, u32[]{:S(2)}) async-start(bf16[4,128,128]{2,1,0:T(8,128)(2,1)} %broadcast_in_dim.13), calls=%async_computation.3 | async-start | bytes 262144 | tf_op jit(solution)/shard_map/all_to_all | solution.py:193
  170.3 0.7 copy-start.3
  171.0 0.7 copy-start.5
  171.7 0.7 copy-start.7
  172.5 29.6 %collective-permute-start.17 = (bf16[4,1024,128]{2,1,0:T(8,128)(2,1)}, bf16[4,1024,128]{2,1,0:T(8,128)(2,1)S(1)}, u32[]{:S(2)}, u32[]{:S(2)}) collective-permute-start(bf16[4,1024,128]{2,1,0:T(8,128)(2,1)} %pad_maximum_fusion), channel_id=1, source_target_pairs={{0,1},{1,0},{2,3},{3,2},{4,5},{5,4},{6,7},{7,6},{8,9},{9,8},{10,11... | collective-permute-start | bytes 3145736 | tf_op jit(solution)/shard_map/ppermute | solution.py:25
  174.4 27.7 %collective-permute-start = (bf16[8,4,128,128]{3,2,1,0:T(8,128)(2,1)S(1)}, bf16[8,4,128,128]{3,2,1,0:T(8,128)(2,1)S(1)}, u32[]{:S(2)}, u32[]{:S(2)}) collective-permute-start(bf16[8,4,128,128]{3,2,1,0:T(8,128)(2,1)S(1)} %all-to-all-done.1.weight), channel_id=1, source_target_pairs={{0,1},{1,0},{2,3},{3,2},{4,5},{5,4},{6,7},{7,6},{8,9},{9,8},{10,11... | collective-permute-start | bytes 3145736 | tf_op jit(solution)/shard_map/ppermute | solution.py:25
  177.7 9.7 %collective-permute-start.18 = (bf16[128,128]{1,0:T(8,128)(2,1)S(1)}, bf16[128,128]{1,0:T(8,128)(2,1)S(1)}, u32[]{:S(2)}, u32[]{:S(2)}) collective-permute-start(bf16[128,128]{1,0:T(8,128)(2,1)S(1)} %reduce_sum.25), channel_id=1, source_target_pairs={{0,256},{8,264},{16,272},{24,280},{32,288},{40,296},{48,304},{56,3... | collective-permute-start | bytes 98312 | tf_op jit(solution)/shard_map/ppermute | solution.py:245
  187.5 14.6 %copy-start.8 = (bf16[1024,128]{1,0:T(8,128)(2,1)S(1)}, bf16[1024,128]{1,0:T(8,128)(2,1)}, u32[]{:S(2)}) copy-start(bf16[1024,128]{1,0:T(8,128)(2,1)} %copy-done.7) | copy-start | bytes 786436
  187.5 14.6 %copy-start.11 = (bf16[1024,128]{1,0:T(8,128)(2,1)S(1)}, bf16[1024,128]{1,0:T(8,128)(2,1)}, u32[]{:S(2)}) copy-start(bf16[1024,128]{1,0:T(8,128)(2,1)} %copy-done.10) | copy-start | bytes 786436
  201.3 1.0 copy-start.2
  201.3 1.2 copy-start.4
  201.3 1.3 copy-start.6
where the time goes:
time: 207 us; the launch traced here: 206 us
  starting transfers between devices  82.4 us (40%)
  waiting for transfers between devices  80.2 us (39%)
  blocking collectives  13.7 us (7%)
  Pallas kernels  10.9 us (5%)
  local copies, waits for them, and re-layouts  10.7 us (5%)
  other arithmetic  6.44 us (3%)
    all_to_all x3, waiting for transfers between devices, over_row(): return lax.all_to_all(x, 'row', 0, 0, tiled=True, axis_index_groups=groups)  33.8 us
    ppermute x9, waiting for transfers between devices, rotate(): return lax.ppermute(x, 'col', pairs)  30.9 us
    ppermute x9, starting transfers between devices, rotate(): return lax.ppermute(x, 'col', pairs)  24.2 us
    all_to_all x3, starting transfers between devices, over_row(): return lax.all_to_all(x, 'row', 0, 0, tiled=True, axis_index_groups=groups)  21.8 us
    ppermute x7, starting transfers between devices, swap(): lax.ppermute(x, 'col', [(i, i ^ 1) for i in range(lax.axis_size('col'))])  14.9 us
    all_to_all x1, blocking collectives, over_row(): return lax.all_to_all(x, 'row', 0, 0, tiled=True, axis_index_groups=groups)  13.7 us
    ppermute x2, starting transfers between devices, paired(): return lax.ppermute(x, axis, pairs + [(j, i) for i, j in pairs])  12.8 us
    unnamed x44, local copies, waits for them, and re-layouts  8.54 us
  transfers between devices with their start and end apart: 23, of which 9 were waited for; matrix products, arithmetic and copies ran while one was open for 3% of the time, Pallas kernels for 1%

commit v1 on v0

--- a/solution.py
+++ b/solution.py
@@ -35,7 +35,10 @@
 def gather(x):
     chips = lax.axis_size("col") // CORES
     same = [x] + [rotate(x, by) for by in range(1, chips)]
-    return same + [swap(block) for block in same]
+    swapped = []
+    for block in same:
+        swapped.append(swap(block))
+    return same + swapped
 
 
 def origins(me, chips):
@@ -120,16 +123,27 @@
             out[at : at + step, :] = total.astype(BF16)
 
 
+def pair_kernel(mine, other, kept, *ahead):
+    slab = kept.shape[0]
+    kept[...] = mine[:slab, :].astype(F32) + other[:slab, :].astype(F32)
+    for at, out in enumerate(ahead, 1):
+        here = slice(at * slab, (at + 1) * slab)
+        out[...] = (mine[here, :].astype(F32) + other[here, :].astype(F32)).astype(BF16)
+
+
 def main_kernel(where, packed, weight, *refs):
-    *aggs, grads, parts = refs
+    *aggs, grads, parts, other_scale = refs
     slab, width = aggs[0].shape
     pieces = parts.shape[0]
     rows = lax.broadcasted_iota(jnp.int32, (slab, slab), 0)
     eye = rows == lax.broadcasted_iota(jnp.int32, (slab, slab), 1)
     total = None
-    for at, agg in zip(origins(where[0], len(aggs) // CORES), aggs):
+    chips = len(aggs) // CORES
+    for place, (at, agg) in enumerate(zip(origins(where[0], chips), aggs)):
         degree = packed[at, packed.shape[1] - PAD :, :][:1, :].astype(F32)
         scale = jnp.sum(jnp.where(eye, 1.0 / jnp.sqrt(degree), 0.0), axis=1, keepdims=True)
+        if place == chips:
+            other_scale[...] = scale
         pre = jnp.dot(agg[...], weight[...], preferred_element_type=F32) * scale
         sig = jax.nn.sigmoid(pre)
         slope = sig * (1.0 + pre * (1.0 - sig))
@@ -144,31 +158,50 @@
         parts[at] = total[:, at * (width // pieces) : (at + 1) * (width // pieces)]
 
 
-def final_kernel(where, weight, other, agg, middle, scale, *refs):
-    *same, others, layer_out, out, mixed, whole = refs
+def final_kernel(where, weight, agg, other_agg, middle, other_middle, scale, other_scale, *refs):
+    *grads, lines, out, theirs, mixed, whole = refs
     outer, chips, depth, cols = weight.shape
-    for blocks, core in ((weight, where[0] % CORES), (other, 1 - where[0] % CORES)):
-        for chip in range(chips):
-            here = pl.ds(pl.multiple_of((chip * CORES + core) * cols, cols), cols)
-            for step in range(outer):
-                whole[step * depth : (step + 1) * depth, here] = blocks[step, chip]
+    slab, width = out.shape
+    for at in range(chips):
+        for step in range(outer):
+            here = slice(step * depth, (step + 1) * depth)
+            whole[here, at * cols : (at + 1) * cols] = weight[step, at]
+    for rows, factor, target, base in (
+        (agg, scale, lines, 0),
+        (other_agg, other_scale, theirs, width),
+    ):
+        pre = jnp.dot(rows[...], whole[...], preferred_element_type=F32) * factor[...]
+        target[:, base : base + chips * cols] = (pre * jax.nn.sigmoid(pre)).astype(BF16)
+    chip = where[0] // CORES
+    for by, grad in enumerate(grads):
+        at = (chip - by + chips) % chips
+        here = pl.ds(pl.multiple_of(at * cols, cols), cols)
+        for place, block in enumerate((middle, other_middle)):
+            part = lax.dot_general(
+                block[...], grad[...], (((0,), (0,)), ((), ())), preferred_element_type=F32
+            )
+            mixed[place * slab : (place + 1) * slab, here] = part.astype(BF16)
     step = 256
-    for at in range(0, out.shape[1], step):
-        here = slice(at, at + step)
-        pre = jnp.dot(agg[...], whole[:, here], preferred_element_type=F32) * scale[...]
-        layer_out[:, here] = (pre * jax.nn.sigmoid(pre)).astype(BF16)
-    grads = [*same, *[others.at[at] for at in range(chips)]]
-    for at, grad in zip(origins(where[0], chips), grads):
-        part = lax.dot_general(
-            middle[...], grad[...], (((0,), (0,)), ((), ())), preferred_element_type=F32
-        )
-        mixed[:, pl.ds(pl.multiple_of(at * cols, cols), cols)] = part.astype(BF16)
-    for at in range(0, out.shape[1], step):
+    for at in range(0, width, step):
         here = slice(at, at + step)
         back = lax.dot_general(
             mixed[...], whole[here, :], (((1,), (1,)), ((), ())), preferred_element_type=F32
         )
-        out[:, here] = (back * scale[...]).astype(BF16)
+        out[:, here] = back[:slab]
+        theirs[:, here] = back[slab:].astype(BF16)
+
+
+def finish_kernel(where, lines, back, arrived, scale, layer_out, out):
+    _, width = out.shape
+    core = where[0] % CORES
+    cols = TILE
+    out[...] = ((back[...] + arrived[:, :width].astype(F32)) * scale[...]).astype(BF16)
+    for at in range(lines.shape[1] // cols):
+        here = slice(at * cols, (at + 1) * cols)
+        mine = pl.ds(pl.multiple_of((at * CORES + core) * cols, cols), cols)
+        other = pl.ds(pl.multiple_of((at * CORES + 1 - core) * cols, cols), cols)
+        layer_out[:, mine] = lines[:, here]
+        layer_out[:, other] = arrived[:, width + at * cols : width + (at + 1) * cols]
 
 
 def per_device(features, history, degree, adj_tiles, tile_index, tile_count, weight, cotangent):
@@ -216,29 +249,32 @@
         flops=6 * part_rows * slab * width,
     )(block, first, own, second)
     other = swap(theirs)
-    arrived = []
-    for by in range(1, chips):
-        here = slice(by * slab, (by + 1) * slab)
-        ahead = (mine[here].astype(F32) + other[here].astype(F32)).astype(BF16)
-        arrived.append(rotate(ahead, by))
-    agg = mine[:slab].astype(F32) + other[:slab].astype(F32)
-    agg = (agg + sum(block.astype(F32) for block in arrived)).astype(BF16)
+    kept, *ahead = call(
+        pair_kernel, [((slab, width), F32)] + [((slab, width), BF16)] * (chips - 1), (0, 2)
+    )(mine, other)
+    arrived = [rotate(block, by) for by, block in enumerate(ahead, 1)]
+    agg = (kept + sum(block.astype(F32) for block in arrived)).astype(BF16)
     core = where[0] % CORES
     mine_cols = packed.reshape(chips, CORES, slab + depth + PAD, out_cols)
     mine_cols = lax.dynamic_index_in_dim(mine_cols, core, 1, keepdims=False)
     half_weight = replicated(mine_cols[:, slab : slab + depth, :], near)
-    other_weight = swap(half_weight)
+    other_middle = swap(middle)
     aggs = gather(agg)
-    grad, parts = call(
+    grad, parts, other_scale = call(
         main_kernel,
-        [((part_rows, out_cols), BF16), ((RING, out_cols, depth), BF16)],
+        [
+            ((part_rows, out_cols), BF16),
+            ((RING, out_cols, depth), BF16),
+            ((slab, 1), F32),
+        ],
         (1, 2 + cols),
         flops=4 * part_rows * width * out_cols,
         transcendentals=part_rows * out_cols,
     )(where, packed, weight, *aggs)
     summed = over_row(parts, near)
-    grads = [grad] + [rotate(grad, by) for by in range(1, chips)]
-    others = swap(jnp.stack(grads))
+    grads = [grad]
+    for by in range(1, chips):
+        grads.append(rotate(grad, by))
     summed = total(summed).T.astype(BF16)
     summed = replicated(summed, across)
     summed = total(summed).astype(BF16)
@@ -247,14 +283,19 @@
     summed = summed * (1.0 / math.sqrt(part_rows * rows))
     summed = replicated(summed.astype(BF16), near)
     grad_weight = summed.reshape(width, out_cols).astype(F32)
-    layer_out, grad_features = call(
+    own_cols = chips * out_cols
+    lines, back, theirs = call(
         final_kernel,
-        [((slab, width), BF16)] * 2,
-        (1, 6 + chips),
-        [pltpu.VMEM((slab, width), BF16), pltpu.VMEM((width, width), BF16)],
+        [((slab, own_cols), BF16), ((slab, width), F32), ((slab, width + own_cols), BF16)],
+        (1, 7 + chips),
+        [pltpu.VMEM((CORES * slab, own_cols), BF16), pltpu.VMEM((width, own_cols), BF16)],
         flops=6 * slab * width * width,
         transcendentals=slab * width,
-    )(where, half_weight, other_weight, agg, middle, scale, *grads, others)
+    )(where, half_weight, agg, aggs[chips], middle, other_middle, scale, other_scale, *grads)
+    arrived = swap(theirs)
+    layer_out, grad_features = call(
+        finish_kernel, [((slab, width), BF16)] * 2, (1, 4)
+    )(where, lines, back, arrived, scale)
     return layer_out, grad_features, grad_weight
 
 

time: 207 us -> 192 us (0.928)
  the two profiles are of different devices: /device:TPU:26 before, /device:TPU:24 now
where the time goes in v1:
time: 192 us; the launch traced here: 190 us
  waiting for transfers between devices  83.2 us (43%)
  starting transfers between devices  82.6 us (43%)
  Pallas kernels  12.6 us (7%)
  local copies, waits for them, and re-layouts  6.51 us (3%)
  other arithmetic  3.86 us (2%)
    all_to_all x4, waiting for transfers between devices, over_row(): return lax.all_to_all(x, 'row', 0, 0, tiled=True, axis_index_groups=groups)  39.2 us
    ppermute x9, waiting for transfers between devices, rotate(): return lax.ppermute(x, 'col', pairs)  36.7 us
    all_to_all x4, starting transfers between devices, over_row(): return lax.all_to_all(x, 'row', 0, 0, tiled=True, axis_index_groups=groups)  26.9 us
    ppermute x9, starting transfers between devices, rotate(): return lax.ppermute(x, 'col', pairs)  24.3 us
    ppermute x7, starting transfers between devices, swap(): lax.ppermute(x, 'col', [(i, i ^ 1) for i in range(lax.axis_size('col'))])  14 us
    ppermute x2, starting transfers between devices, paired(): return lax.ppermute(x, axis, pairs + [(j, i) for i, j in pairs])  8.56 us
    all_to_all x1, starting transfers between devices, per_device(): packed = lax.all_to_all(packed, 'col', 0, 0, tiled=True)  6.85 us
  transfers between devices with their start and end apart: 24, of which 10 were waited for; matrix products, arithmetic and copies ran while one was open for 2% of the time, Pallas kernels for 3%

profile of v1, /device:TPU:24, one launch (start us, length us, event | category | flops | bytes accessed | tf_op | source)
XLA Modules:
  0.0 190.4 jit_solution(9320377688052086171)
XLA Ops:
  0.6 0.7 convert_rsqrt_fusion
  1.3 1.1 multiply_convert_fusion
  2.4 0.7 collective-permute-start
  3.1 7.9 %collective-permute-start.1 = (bf16[128,1024]{1,0:T(8,128)(2,1)S(1)}, bf16[128,1024]{1,0:T(8,128)(2,1)S(1)}, u32[]{:S(2)}, u32[]{:S(2)}) collective-permute-start(bf16[128,1024]{1,0:T(8,128)(2,1)S(1)} %multiply_convert_fusion), channel_id=1, source_target_pairs={{0,8},{16,24},{32,40},{48,56},{64,72},{80,88},{96,104},{112,120},{... | collective-permute-start | bytes 786440 | tf_op jit(solution)/shard_map/ppermute | solution.py:21
  11.0 0.1 copy.18.scale
  11.8 0.0 copy-start.11
  11.8 0.1 pad_add_fusion.where
  11.9 0.6 copy-done.11
  12.4 0.9 shard_map.104
  13.4 0.0 collective-permute-done.first
  13.4 3.6 %collective-permute-done.1.second = bf16[128,1024]{1,0:T(8,128)(2,1)S(1)} collective-permute-done((bf16[128,1024]{1,0:T(8,128)(2,1)S(1)}, bf16[128,1024]{1,0:T(8,128)(2,1)S(1)}, u32[]{:S(2)}, u32[]{:S(2)}) %collective-permute-start.1) | collective-permute-done | bytes 262176 | tf_op jit(solution)/shard_map/ppermute | solution.py:21
  17.0 1.8 shard_map.105
  18.8 1.9 %collective-permute-start.2 = (bf16[512,1024]{1,0:T(8,128)(2,1)S(1)}, bf16[512,1024]{1,0:T(8,128)(2,1)S(1)}, u32[]{:S(2)}, u32[]{:S(2)}) collective-permute-start(bf16[512,1024]{1,0:T(8,128)(2,1)S(1)} %get-tuple-element.23), channel_id=1, source_target_pairs={{0,1},{1,0},{2,3},{3,2},{4,5},{5,4},{6,7},{7,6},{8,9},{9,8},{10,11... | collective-permute-start | bytes 3145736 | tf_op jit(solution)/shard_map/ppermute | solution.py:25
  20.7 2.6 %collective-permute-done.2.other = bf16[512,1024]{1,0:T(8,128)(2,1)S(1)} collective-permute-done((bf16[512,1024]{1,0:T(8,128)(2,1)S(1)}, bf16[512,1024]{1,0:T(8,128)(2,1)S(1)}, u32[]{:S(2)}, u32[]{:S(2)}) %collective-permute-start.2) | collective-permute-done | bytes 1048608 | tf_op jit(solution)/shard_map/ppermute | solution.py:25
  23.3 0.2 shard_map.106
  23.6 2.1 %collective-permute-start.3 = (bf16[128,1024]{1,0:T(8,128)(2,1)S(1)}, bf16[128,1024]{1,0:T(8,128)(2,1)S(1)}, u32[]{:S(2)}, u32[]{:S(2)}) collective-permute-start(bf16[128,1024]{1,0:T(8,128)(2,1)S(1)} %get-tuple-element.25), channel_id=1, source_target_pairs={{0,2},{1,3},{2,4},{3,5},{4,6},{5,7},{6,0},{7,1},{8,10},{9,11},{10,... | collective-permute-start | bytes 786440 | tf_op jit(solution)/shard_map/ppermute | solution.py:32
  25.7 3.6 %collective-permute-start.4 = (bf16[128,1024]{1,0:T(8,128)(2,1)S(1)}, bf16[128,1024]{1,0:T(8,128)(2,1)S(1)}, u32[]{:S(2)}, u32[]{:S(2)}) collective-permute-start(bf16[128,1024]{1,0:T(8,128)(2,1)S(1)} %get-tuple-element.26), channel_id=1, source_target_pairs={{0,4},{1,5},{2,6},{3,7},{4,0},{5,1},{6,2},{7,3},{8,12},{9,13},{10,... | collective-permute-start | bytes 786440 | tf_op jit(solution)/shard_map/ppermute | solution.py:32
  29.3 0.0 copy-start.10
  29.3 2.4 %collective-permute-start.5 = (bf16[128,1024]{1,0:T(8,128)(2,1)S(1)}, bf16[128,1024]{1,0:T(8,128)(2,1)S(1)}, u32[]{:S(2)}, u32[]{:S(2)}) collective-permute-start(bf16[128,1024]{1,0:T(8,128)(2,1)S(1)} %get-tuple-element.27), channel_id=1, source_target_pairs={{0,6},{1,7},{2,0},{3,1},{4,2},{5,3},{6,4},{7,5},{8,14},{9,15},{10,... | collective-permute-start | bytes 786440 | tf_op jit(solution)/shard_map/ppermute | solution.py:32
  31.7 1.4 shard_map.103
  33.2 6.8 %all-to-all-start = ((bf16[8,272,128]{2,1,0:T(8,128)(2,1)}), bf16[8,272,128]{2,1,0:T(8,128)(2,1)S(1)}, u32[]{:S(2)}, u32[]{:S(2)}) async-start(bf16[8,272,128]{2,1,0:T(8,128)(2,1)} %shard_map.103), calls=%async_computation | async-start | bytes 1114112 | tf_op jit(solution)/shard_map/all_to_all | solution.py:239
  40.0 20.8 %collective-permute-done.4 = bf16[128,1024]{1,0:T(8,128)(2,1)S(1)} collective-permute-done((bf16[128,1024]{1,0:T(8,128)(2,1)S(1)}, bf16[128,1024]{1,0:T(8,128)(2,1)S(1)}, u32[]{:S(2)}, u32[]{:S(2)}) %collective-permute-start.4) | collective-permute-done | bytes 262176 | tf_op jit(solution)/shard_map/ppermute | solution.py:32
  60.8 0.0 collective-permute-done.5
  60.8 0.1 add_convert_fusion.refs_0_.agg
  61.0 1.9 %collective-permute-start.8 = (bf16[128,1024]{1,0:T(8,128)(2,1)S(1)}, bf16[128,1024]{1,0:T(8,128)(2,1)S(1)}, u32[]{:S(2)}, u32[]{:S(2)}) collective-permute-start(bf16[128,1024]{1,0:T(8,128)(2,1)S(1)} %add_convert_fusion.refs_0_.agg), channel_id=1, source_target_pairs={{0,2},{1,3},{2,4},{3,5},{4,6},{5,7},{6,0},{7,1},{8,10},{9,11},{10,... | collective-permute-start | bytes 786440 | tf_op jit(solution)/shard_map/ppermute | solution.py:32
  62.9 2.6 %collective-permute-start.9 = (bf16[128,1024]{1,0:T(8,128)(2,1)S(1)}, bf16[128,1024]{1,0:T(8,128)(2,1)S(1)}, u32[]{:S(2)}, u32[]{:S(2)}) collective-permute-start(bf16[128,1024]{1,0:T(8,128)(2,1)S(1)} %add_convert_fusion.refs_0_.agg), channel_id=1, source_target_pairs={{0,4},{1,5},{2,6},{3,7},{4,0},{5,1},{6,2},{7,3},{8,12},{9,13},{10,... | collective-permute-start | bytes 786440 | tf_op jit(solution)/shard_map/ppermute | solution.py:32
  65.5 3.9 %collective-permute-start.10 = (bf16[128,1024]{1,0:T(8,128)(2,1)S(1)}, bf16[128,1024]{1,0:T(8,128)(2,1)S(1)}, u32[]{:S(2)}, u32[]{:S(2)}) collective-permute-start(bf16[128,1024]{1,0:T(8,128)(2,1)S(1)} %add_convert_fusion.refs_0_.agg), channel_id=1, source_target_pairs={{0,6},{1,7},{2,0},{3,1},{4,2},{5,3},{6,4},{7,5},{8,14},{9,15},{10,... | collective-permute-start | bytes 786440 | tf_op jit(solution)/shard_map/ppermute | solution.py:32
  69.4 1.9 %collective-permute-start.6 = (bf16[128,1024]{1,0:T(8,128)(2,1)S(1)}, bf16[128,1024]{1,0:T(8,128)(2,1)S(1)}, u32[]{:S(2)}, u32[]{:S(2)}) collective-permute-start(bf16[128,1024]{1,0:T(8,128)(2,1)S(1)} %add_convert_fusion.refs_0_.agg), channel_id=1, source_target_pairs={{0,1},{1,0},{2,3},{3,2},{4,5},{5,4},{6,7},{7,6},{8,9},{9,8},{10,11... | collective-permute-start | bytes 786440 | tf_op jit(solution)/shard_map/ppermute | solution.py:25
  71.3 0.9 collective-permute-done.8.refs_1_
  72.3 1.9 %collective-permute-start.11 = (bf16[128,1024]{1,0:T(8,128)(2,1)S(1)}, bf16[128,1024]{1,0:T(8,128)(2,1)S(1)}, u32[]{:S(2)}, u32[]{:S(2)}) collective-permute-start(bf16[128,1024]{1,0:T(8,128)(2,1)S(1)} %collective-permute-done.8.refs_1_), channel_id=1, source_target_pairs={{0,1},{1,0},{2,3},{3,2},{4,5},{5,4},{6,7},{7,6},{8,9},{9,8},{10,11... | collective-permute-start | bytes 786440 | tf_op jit(solution)/shard_map/ppermute | solution.py:25
  74.2 14.9 %collective-permute-done.9.refs_2_ = bf16[128,1024]{1,0:T(8,128)(2,1)S(1)} collective-permute-done((bf16[128,1024]{1,0:T(8,128)(2,1)S(1)}, bf16[128,1024]{1,0:T(8,128)(2,1)S(1)}, u32[]{:S(2)}, u32[]{:S(2)}) %collective-permute-start.9) | collective-permute-done | bytes 262176 | tf_op jit(solution)/shard_map/ppermute | solution.py:32
  89.1 1.9 %collective-permute-start.12 = (bf16[128,1024]{1,0:T(8,128)(2,1)S(1)}, bf16[128,1024]{1,0:T(8,128)(2,1)S(1)}, u32[]{:S(2)}, u32[]{:S(2)}) collective-permute-start(bf16[128,1024]{1,0:T(8,128)(2,1)S(1)} %collective-permute-done.9.refs_2_), channel_id=1, source_target_pairs={{0,1},{1,0},{2,3},{3,2},{4,5},{5,4},{6,7},{7,6},{8,9},{9,8},{10,11... | collective-permute-start | bytes 786440 | tf_op jit(solution)/shard_map/ppermute | solution.py:25
  91.1 2.4 %collective-permute-start.13 = (bf16[128,1024]{1,0:T(8,128)(2,1)S(1)}, bf16[128,1024]{1,0:T(8,128)(2,1)S(1)}, u32[]{:S(2)}, u32[]{:S(2)}) collective-permute-start(bf16[128,1024]{1,0:T(8,128)(2,1)S(1)} %collective-permute-done.10.refs_3_), channel_id=1, source_target_pairs={{0,1},{1,0},{2,3},{3,2},{4,5},{5,4},{6,7},{7,6},{8,9},{9,8},{10,11... | collective-permute-start | bytes 786440 | tf_op jit(solution)/shard_map/ppermute | solution.py:25
  93.5 0.0 collective-permute-done.11.refs_5_
  93.5 0.0 collective-permute-done.12.refs_6_
  93.5 1.1 collective-permute-done.13.refs_7_
  94.6 3.8 %shard_map.107 = (bf16[1024,128]{1,0:T(8,128)(2,1)S(1)}, bf16[8,128,128]{2,1,0:T(8,128)(2,1)}, f32[128,1]{1,0:T(8,128)S(1)}) custom-call(s32[2]{0:T(128)S(1)} %pad_add_fusion.where, bf16[8,272,128]{2,1,0:T(8,128)(2,1)S(1)} %all-to-all-done.packed, bf16[1024,128]{1,0:T(8,128)(2,1)S(1)} %copy-done, bf16[128,1024]{1,0:T(8,128)(2,1)S(1)} %add_convert_fusion.refs_0_.agg, ...), custom_call_target="tpu_custom_call" | custom-call | flops 536870912 | bytes 2097152 | tf_op jit(solution)/shard_map/pallas_call | solution.py:263
  98.4 0.7 copy-done.3
  99.1 4.6 %all-to-all-start.2 = ((bf16[8,128,128]{2,1,0:T(8,128)(2,1)}), bf16[8,128,128]{2,1,0:T(8,128)(2,1)S(1)}, u32[]{:S(2)}, u32[]{:S(2)}) async-start(bf16[8,128,128]{2,1,0:T(8,128)(2,1)} %get-tuple-element.36), calls=%async_computation.2 | async-start | bytes 524288 | tf_op jit(solution)/shard_map/all_to_all | solution.py:226
  103.8 12.4 %all-to-all-done.2 = bf16[8,128,128]{2,1,0:T(8,128)(2,1)S(1)} async-done(((bf16[8,128,128]{2,1,0:T(8,128)(2,1)}), bf16[8,128,128]{2,1,0:T(8,128)(2,1)S(1)}, u32[]{:S(2)}, u32[]{:S(2)}) %all-to-all-start.2) | async-done | bytes 262176 | tf_op jit(solution)/shard_map/all_to_all | solution.py:226
  116.2 0.1 copy.21
  116.3 0.7 broadcast_in_dim.13
  117.0 14.6 %all-to-all-start.3 = ((bf16[4,128,128]{2,1,0:T(8,128)(2,1)}), bf16[4,128,128]{2,1,0:T(8,128)(2,1)S(1)}, u32[]{:S(2)}, u32[]{:S(2)}) async-start(bf16[4,128,128]{2,1,0:T(8,128)(2,1)} %broadcast_in_dim.13), calls=%async_computation.3 | async-start | bytes 262144 | tf_op jit(solution)/shard_map/all_to_all | solution.py:226
  131.6 5.9 %all-to-all-done.3 = bf16[4,128,128]{2,1,0:T(8,128)(2,1)S(1)} async-done(((bf16[4,128,128]{2,1,0:T(8,128)(2,1)}), bf16[4,128,128]{2,1,0:T(8,128)(2,1)S(1)}, u32[]{:S(2)}, u32[]{:S(2)}) %all-to-all-start.3) | async-done | bytes 131104 | tf_op jit(solution)/shard_map/all_to_all | solution.py:226
  137.6 1.2 broadcast_in_dim.11
  138.8 3.7 %all-to-all-start.1 = ((bf16[8,4,128,128]{3,2,1,0:T(8,128)(2,1)}), bf16[8,4,128,128]{3,2,1,0:T(8,128)(2,1)S(1)}, u32[]{:S(2)}, u32[]{:S(2)}) async-start(bf16[8,4,128,128]{3,2,1,0:T(8,128)(2,1)} %broadcast_in_dim.11), calls=%async_computation.1 | async-start | bytes 2097152 | tf_op jit(solution)/shard_map/all_to_all | solution.py:226
  142.5 1.9 %collective-permute-start.18 = (bf16[128,128]{1,0:T(8,128)(2,1)S(1)}, bf16[128,128]{1,0:T(8,128)(2,1)S(1)}, u32[]{:S(2)}, u32[]{:S(2)}) collective-permute-start(bf16[128,128]{1,0:T(8,128)(2,1)S(1)} %reduce_sum.25), channel_id=1, source_target_pairs={{0,256},{8,264},{16,272},{24,280},{32,288},{40,296},{48,304},{56,3... | collective-permute-start | bytes 98312 | tf_op jit(solution)/shard_map/ppermute | solution.py:281
  144.4 1.9 %collective-permute-start.7 = (bf16[1024,128]{1,0:T(8,128)(2,1)S(1)}, bf16[1024,128]{1,0:T(8,128)(2,1)S(1)}, u32[]{:S(2)}, u32[]{:S(2)}) collective-permute-start(bf16[1024,128]{1,0:T(8,128)(2,1)S(1)} %get-tuple-element.28.middle), channel_id=1, source_target_pairs={{0,1},{1,0},{2,3},{3,2},{4,5},{5,4},{6,7},{7,6},{8,9},{9,8},{10,11... | collective-permute-start | bytes 786440 | tf_op jit(solution)/shard_map/ppermute | solution.py:25
  146.4 1.9 %collective-permute-start.14 = (bf16[1024,128]{1,0:T(8,128)(2,1)S(1)}, bf16[1024,128]{1,0:T(8,128)(2,1)S(1)}, u32[]{:S(2)}, u32[]{:S(2)}) collective-permute-start(bf16[1024,128]{1,0:T(8,128)(2,1)S(1)} %copy-done.4), channel_id=1, source_target_pairs={{0,2},{1,3},{2,4},{3,5},{4,6},{5,7},{6,0},{7,1},{8,10},{9,11},{10,... | collective-permute-start | bytes 786440 | tf_op jit(solution)/shard_map/ppermute | solution.py:32
  148.3 1.9 %collective-permute-start.15 = (bf16[1024,128]{1,0:T(8,128)(2,1)S(1)}, bf16[1024,128]{1,0:T(8,128)(2,1)S(1)}, u32[]{:S(2)}, u32[]{:S(2)}) collective-permute-start(bf16[1024,128]{1,0:T(8,128)(2,1)S(1)} %copy-done.4), channel_id=1, source_target_pairs={{0,4},{1,5},{2,6},{3,7},{4,0},{5,1},{6,2},{7,3},{8,12},{9,13},{10,... | collective-permute-start | bytes 786440 | tf_op jit(solution)/shard_map/ppermute | solution.py:32
  150.2 3.9 %collective-permute-start.16 = (bf16[1024,128]{1,0:T(8,128)(2,1)S(1)}, bf16[1024,128]{1,0:T(8,128)(2,1)S(1)}, u32[]{:S(2)}, u32[]{:S(2)}) collective-permute-start(bf16[1024,128]{1,0:T(8,128)(2,1)S(1)} %copy-done.4), channel_id=1, source_target_pairs={{0,6},{1,7},{2,0},{3,1},{4,2},{5,3},{6,4},{7,5},{8,14},{9,15},{10,... | collective-permute-start | bytes 786440 | tf_op jit(solution)/shard_map/ppermute | solution.py:32
  154.2 15.9 %all-to-all-done.1.weight = bf16[8,4,128,128]{3,2,1,0:T(8,128)(2,1)S(1)} async-done(((bf16[8,4,128,128]{3,2,1,0:T(8,128)(2,1)}), bf16[8,4,128,128]{3,2,1,0:T(8,128)(2,1)S(1)}, u32[]{:S(2)}, u32[]{:S(2)}) %all-to-all-start.1) | async-done | bytes 1048608 | tf_op jit(solution)/shard_map/all_to_all | solution.py:226
  170.1 0.7 broadcast_in_dim.28
  170.8 4.1 %all-to-all-start.4 = ((bf16[8,128,128]{2,1,0:T(8,128)(2,1)}), bf16[8,128,128]{2,1,0:T(8,128)(2,1)}, u32[]{:S(2)}, u32[]{:S(2)}) async-start(bf16[8,128,128]{2,1,0:T(8,128)(2,1)} %broadcast_in_dim.28), calls=%async_computation.4 | async-start | bytes 524288 | tf_op jit(solution)/shard_map/all_to_all | solution.py:226
  174.9 0.0 collective-permute-done.14.refs_1_
  174.9 0.0 copy-start.5
  175.0 0.7 copy-done.5
  175.7 0.9 copy-done.6
  176.6 3.0 %shard_map.108 = (bf16[128,512]{1,0:T(8,128)(2,1)S(1)}, f32[128,1024]{1,0:T(8,128)S(1)}, bf16[128,1536]{1,0:T(8,128)(2,1)}) custom-call(s32[2]{0:T(128)S(1)} %pad_add_fusion.where, bf16[8,4,128,128]{3,2,1,0:T(8,128)(2,1)S(1)} %all-to-all-done.1.weight, bf16[128,1024]{1,0:T(8,128)(2,1)S(1)} %add_convert_fusion.refs_0_.agg, ...), custom_call_target="tpu_custom_call" | custom-call | flops 805306368 | bytes 2097152 | tf_op jit(solution)/shard_map/pallas_call | solution.py:287
  179.6 0.7 copy-done.8
  180.2 2.0 %collective-permute-start.17 = (bf16[128,1536]{1,0:T(8,128)(2,1)}, bf16[128,1536]{1,0:T(8,128)(2,1)S(1)}, u32[]{:S(2)}, u32[]{:S(2)}) collective-permute-start(bf16[128,1536]{1,0:T(8,128)(2,1)} %get-tuple-element.33), channel_id=1, source_target_pairs={{0,1},{1,0},{2,3},{3,2},{4,5},{5,4},{6,7},{7,6},{8,9},{9,8},{10,11... | collective-permute-start | bytes 1179656 | tf_op jit(solution)/shard_map/ppermute | solution.py:25
  182.3 4.9 %all-to-all-done.4 = bf16[8,128,128]{2,1,0:T(8,128)(2,1)} async-done(((bf16[8,128,128]{2,1,0:T(8,128)(2,1)}), bf16[8,128,128]{2,1,0:T(8,128)(2,1)}, u32[]{:S(2)}, u32[]{:S(2)}) %all-to-all-start.4) | async-done | bytes 262176 | tf_op jit(solution)/shard_map/all_to_all | solution.py:226
  187.2 1.8 bitcast_convert_fusion
  189.0 1.4 shard_map.109
  (30 shorter events, 0.2 us)
Async XLA Ops:
  1.3 10.6 %copy-start.2 = (bf16[128,1024]{1,0:T(8,128)(2,1)S(1)}, bf16[128,1024]{1,0:T(8,128)(2,1)}, u32[]{:S(2)}) copy-start(bf16[128,1024]{1,0:T(8,128)(2,1)} %feats.1) | copy-start | bytes 786436
  1.3 10.6 %copy-start.7 = (bf16[6,128,128]{2,1,0:T(8,128)(2,1)S(1)}, bf16[6,128,128]{2,1,0:T(8,128)(2,1)}, u32[]{:S(2)}) copy-start(bf16[6,128,128]{2,1,0:T(8,128)(2,1)} %tiles.1) | copy-start | bytes 589828
  2.4 10.9 %collective-permute-start = (bf16[128,1024]{1,0:T(8,128)(2,1)S(1)}, bf16[128,1024]{1,0:T(8,128)(2,1)S(1)}, u32[]{:S(2)}, u32[]{:S(2)}) collective-permute-start(bf16[128,1024]{1,0:T(8,128)(2,1)S(1)} %multiply_convert_fusion), channel_id=1, source_target_pairs={{8,16},{24,32},{40,48},{56,64},{72,80},{88,96},{104,112},{120,128}... | collective-permute-start | bytes 786440 | tf_op jit(solution)/shard_map/ppermute | solution.py:21
  3.1 13.9 %collective-permute-start.1 = (bf16[128,1024]{1,0:T(8,128)(2,1)S(1)}, bf16[128,1024]{1,0:T(8,128)(2,1)S(1)}, u32[]{:S(2)}, u32[]{:S(2)}) collective-permute-start(bf16[128,1024]{1,0:T(8,128)(2,1)S(1)} %multiply_convert_fusion), channel_id=1, source_target_pairs={{0,8},{16,24},{32,40},{48,56},{64,72},{80,88},{96,104},{112,120},{... | collective-permute-start | bytes 786440 | tf_op jit(solution)/shard_map/ppermute | solution.py:21
  11.8 0.7 copy-start.11
  18.8 4.6 %collective-permute-start.2 = (bf16[512,1024]{1,0:T(8,128)(2,1)S(1)}, bf16[512,1024]{1,0:T(8,128)(2,1)S(1)}, u32[]{:S(2)}, u32[]{:S(2)}) collective-permute-start(bf16[512,1024]{1,0:T(8,128)(2,1)S(1)} %get-tuple-element.23), channel_id=1, source_target_pairs={{0,1},{1,0},{2,3},{3,2},{4,5},{5,4},{6,7},{7,6},{8,9},{9,8},{10,11... | collective-permute-start | bytes 3145736 | tf_op jit(solution)/shard_map/ppermute | solution.py:25
  23.3 8.4 %copy-start = (bf16[1024,128]{1,0:T(8,128)(2,1)S(1)}, bf16[1024,128]{1,0:T(8,128)(2,1)}, u32[]{:S(2)}) copy-start(bf16[1024,128]{1,0:T(8,128)(2,1)} %weight.3) | copy-start | bytes 786436
  23.3 8.4 %copy-start.1 = (bf16[128,1024]{1,0:T(8,128)(2,1)S(1)}, bf16[128,1024]{1,0:T(8,128)(2,1)}, u32[]{:S(2)}) copy-start(bf16[128,1024]{1,0:T(8,128)(2,1)} %cot.1) | copy-start | bytes 786436
  23.6 16.4 %collective-permute-start.3 = (bf16[128,1024]{1,0:T(8,128)(2,1)S(1)}, bf16[128,1024]{1,0:T(8,128)(2,1)S(1)}, u32[]{:S(2)}, u32[]{:S(2)}) collective-permute-start(bf16[128,1024]{1,0:T(8,128)(2,1)S(1)} %get-tuple-element.25), channel_id=1, source_target_pairs={{0,2},{1,3},{2,4},{3,5},{4,6},{5,7},{6,0},{7,1},{8,10},{9,11},{10,... | collective-permute-start | bytes 786440 | tf_op jit(solution)/shard_map/ppermute | solution.py:32
  25.7 35.1 %collective-permute-start.4 = (bf16[128,1024]{1,0:T(8,128)(2,1)S(1)}, bf16[128,1024]{1,0:T(8,128)(2,1)S(1)}, u32[]{:S(2)}, u32[]{:S(2)}) collective-permute-start(bf16[128,1024]{1,0:T(8,128)(2,1)S(1)} %get-tuple-element.26), channel_id=1, source_target_pairs={{0,4},{1,5},{2,6},{3,7},{4,0},{5,1},{6,2},{7,3},{8,12},{9,13},{10,... | collective-permute-start | bytes 786440 | tf_op jit(solution)/shard_map/ppermute | solution.py:32
  29.3 2.4 %copy-start.10 = (s32[128]{0:T(128)S(1)}, s32[128]{0:T(128)}, u32[]{:S(2)}) copy-start(s32[128]{0:T(128)} %param.10) | copy-start | bytes 1540
  29.3 31.5 %collective-permute-start.5 = (bf16[128,1024]{1,0:T(8,128)(2,1)S(1)}, bf16[128,1024]{1,0:T(8,128)(2,1)S(1)}, u32[]{:S(2)}, u32[]{:S(2)}) collective-permute-start(bf16[128,1024]{1,0:T(8,128)(2,1)S(1)} %get-tuple-element.27), channel_id=1, source_target_pairs={{0,6},{1,7},{2,0},{3,1},{4,2},{5,3},{6,4},{7,5},{8,14},{9,15},{10,... | collective-permute-start | bytes 786440 | tf_op jit(solution)/shard_map/ppermute | solution.py:32
  33.2 60.3 %all-to-all-start = ((bf16[8,272,128]{2,1,0:T(8,128)(2,1)}), bf16[8,272,128]{2,1,0:T(8,128)(2,1)S(1)}, u32[]{:S(2)}, u32[]{:S(2)}) async-start(bf16[8,272,128]{2,1,0:T(8,128)(2,1)} %shard_map.103), calls=%async_computation | async-start | bytes 1114112 | tf_op jit(solution)/shard_map/all_to_all | solution.py:239
  61.0 11.3 %collective-permute-start.8 = (bf16[128,1024]{1,0:T(8,128)(2,1)S(1)}, bf16[128,1024]{1,0:T(8,128)(2,1)S(1)}, u32[]{:S(2)}, u32[]{:S(2)}) collective-permute-start(bf16[128,1024]{1,0:T(8,128)(2,1)S(1)} %add_convert_fusion.refs_0_.agg), channel_id=1, source_target_pairs={{0,2},{1,3},{2,4},{3,5},{4,6},{5,7},{6,0},{7,1},{8,10},{9,11},{10,... | collective-permute-start | bytes 786440 | tf_op jit(solution)/shard_map/ppermute | solution.py:32
  62.9 26.3 %collective-permute-start.9 = (bf16[128,1024]{1,0:T(8,128)(2,1)S(1)}, bf16[128,1024]{1,0:T(8,128)(2,1)S(1)}, u32[]{:S(2)}, u32[]{:S(2)}) collective-permute-start(bf16[128,1024]{1,0:T(8,128)(2,1)S(1)} %add_convert_fusion.refs_0_.agg), channel_id=1, source_target_pairs={{0,4},{1,5},{2,6},{3,7},{4,0},{5,1},{6,2},{7,3},{8,12},{9,13},{10,... | collective-permute-start | bytes 786440 | tf_op jit(solution)/shard_map/ppermute | solution.py:32
  65.5 25.6 %collective-permute-start.10 = (bf16[128,1024]{1,0:T(8,128)(2,1)S(1)}, bf16[128,1024]{1,0:T(8,128)(2,1)S(1)}, u32[]{:S(2)}, u32[]{:S(2)}) collective-permute-start(bf16[128,1024]{1,0:T(8,128)(2,1)S(1)} %add_convert_fusion.refs_0_.agg), channel_id=1, source_target_pairs={{0,6},{1,7},{2,0},{3,1},{4,2},{5,3},{6,4},{7,5},{8,14},{9,15},{10,... | collective-permute-start | bytes 786440 | tf_op jit(solution)/shard_map/ppermute | solution.py:32
  69.4 24.1 %collective-permute-start.6 = (bf16[128,1024]{1,0:T(8,128)(2,1)S(1)}, bf16[128,1024]{1,0:T(8,128)(2,1)S(1)}, u32[]{:S(2)}, u32[]{:S(2)}) collective-permute-start(bf16[128,1024]{1,0:T(8,128)(2,1)S(1)} %add_convert_fusion.refs_0_.agg), channel_id=1, source_target_pairs={{0,1},{1,0},{2,3},{3,2},{4,5},{5,4},{6,7},{7,6},{8,9},{9,8},{10,11... | collective-permute-start | bytes 786440 | tf_op jit(solution)/shard_map/ppermute | solution.py:25
  72.3 21.2 %collective-permute-start.11 = (bf16[128,1024]{1,0:T(8,128)(2,1)S(1)}, bf16[128,1024]{1,0:T(8,128)(2,1)S(1)}, u32[]{:S(2)}, u32[]{:S(2)}) collective-permute-start(bf16[128,1024]{1,0:T(8,128)(2,1)S(1)} %collective-permute-done.8.refs_1_), channel_id=1, source_target_pairs={{0,1},{1,0},{2,3},{3,2},{4,5},{5,4},{6,7},{7,6},{8,9},{9,8},{10,11... | collective-permute-start | bytes 786440 | tf_op jit(solution)/shard_map/ppermute | solution.py:25
  89.1 4.4 %collective-permute-start.12 = (bf16[128,1024]{1,0:T(8,128)(2,1)S(1)}, bf16[128,1024]{1,0:T(8,128)(2,1)S(1)}, u32[]{:S(2)}, u32[]{:S(2)}) collective-permute-start(bf16[128,1024]{1,0:T(8,128)(2,1)S(1)} %collective-permute-done.9.refs_2_), channel_id=1, source_target_pairs={{0,1},{1,0},{2,3},{3,2},{4,5},{5,4},{6,7},{7,6},{8,9},{9,8},{10,11... | collective-permute-start | bytes 786440 | tf_op jit(solution)/shard_map/ppermute | solution.py:25
  91.1 3.6 %collective-permute-start.13 = (bf16[128,1024]{1,0:T(8,128)(2,1)S(1)}, bf16[128,1024]{1,0:T(8,128)(2,1)S(1)}, u32[]{:S(2)}, u32[]{:S(2)}) collective-permute-start(bf16[128,1024]{1,0:T(8,128)(2,1)S(1)} %collective-permute-done.10.refs_3_), channel_id=1, source_target_pairs={{0,1},{1,0},{2,3},{3,2},{4,5},{5,4},{6,7},{7,6},{8,9},{9,8},{10,11... | collective-permute-start | bytes 786440 | tf_op jit(solution)/shard_map/ppermute | solution.py:25
  98.4 0.7 copy-start.3
  99.1 17.0 %all-to-all-start.2 = ((bf16[8,128,128]{2,1,0:T(8,128)(2,1)}), bf16[8,128,128]{2,1,0:T(8,128)(2,1)S(1)}, u32[]{:S(2)}, u32[]{:S(2)}) async-start(bf16[8,128,128]{2,1,0:T(8,128)(2,1)} %get-tuple-element.36), calls=%async_computation.2 | async-start | bytes 524288 | tf_op jit(solution)/shard_map/all_to_all | solution.py:226
  117.0 20.5 %all-to-all-start.3 = ((bf16[4,128,128]{2,1,0:T(8,128)(2,1)}), bf16[4,128,128]{2,1,0:T(8,128)(2,1)S(1)}, u32[]{:S(2)}, u32[]{:S(2)}) async-start(bf16[4,128,128]{2,1,0:T(8,128)(2,1)} %broadcast_in_dim.13), calls=%async_computation.3 | async-start | bytes 262144 | tf_op jit(solution)/shard_map/all_to_all | solution.py:226
  138.8 7.6 %copy-start.4 = (bf16[1024,128]{1,0:T(8,128)(2,1)S(1)}, bf16[1024,128]{1,0:T(8,128)(2,1)}, u32[]{:S(2)}) copy-start(bf16[1024,128]{1,0:T(8,128)(2,1)} %copy-done.3) | copy-start | bytes 786436
  138.8 31.3 %all-to-all-start.1 = ((bf16[8,4,128,128]{3,2,1,0:T(8,128)(2,1)}), bf16[8,4,128,128]{3,2,1,0:T(8,128)(2,1)S(1)}, u32[]{:S(2)}, u32[]{:S(2)}) async-start(bf16[8,4,128,128]{3,2,1,0:T(8,128)(2,1)} %broadcast_in_dim.11), calls=%async_computation.1 | async-start | bytes 2097152 | tf_op jit(solution)/shard_map/all_to_all | solution.py:226
  142.5 11.7 %collective-permute-start.18 = (bf16[128,128]{1,0:T(8,128)(2,1)S(1)}, bf16[128,128]{1,0:T(8,128)(2,1)S(1)}, u32[]{:S(2)}, u32[]{:S(2)}) collective-permute-start(bf16[128,128]{1,0:T(8,128)(2,1)S(1)} %reduce_sum.25), channel_id=1, source_target_pairs={{0,256},{8,264},{16,272},{24,280},{32,288},{40,296},{48,304},{56,3... | collective-permute-start | bytes 98312 | tf_op jit(solution)/shard_map/ppermute | solution.py:281
  144.4 30.5 %collective-permute-start.7 = (bf16[1024,128]{1,0:T(8,128)(2,1)S(1)}, bf16[1024,128]{1,0:T(8,128)(2,1)S(1)}, u32[]{:S(2)}, u32[]{:S(2)}) collective-permute-start(bf16[1024,128]{1,0:T(8,128)(2,1)S(1)} %get-tuple-element.28.middle), channel_id=1, source_target_pairs={{0,1},{1,0},{2,3},{3,2},{4,5},{5,4},{6,7},{7,6},{8,9},{9,8},{10,11... | collective-permute-start | bytes 786440 | tf_op jit(solution)/shard_map/ppermute | solution.py:25
  146.4 28.5 %collective-permute-start.14 = (bf16[1024,128]{1,0:T(8,128)(2,1)S(1)}, bf16[1024,128]{1,0:T(8,128)(2,1)S(1)}, u32[]{:S(2)}, u32[]{:S(2)}) collective-permute-start(bf16[1024,128]{1,0:T(8,128)(2,1)S(1)} %copy-done.4), channel_id=1, source_target_pairs={{0,2},{1,3},{2,4},{3,5},{4,6},{5,7},{6,0},{7,1},{8,10},{9,11},{10,... | collective-permute-start | bytes 786440 | tf_op jit(solution)/shard_map/ppermute | solution.py:32
  148.3 26.6 %collective-permute-start.15 = (bf16[1024,128]{1,0:T(8,128)(2,1)S(1)}, bf16[1024,128]{1,0:T(8,128)(2,1)S(1)}, u32[]{:S(2)}, u32[]{:S(2)}) collective-permute-start(bf16[1024,128]{1,0:T(8,128)(2,1)S(1)} %copy-done.4), channel_id=1, source_target_pairs={{0,4},{1,5},{2,6},{3,7},{4,0},{5,1},{6,2},{7,3},{8,12},{9,13},{10,... | collective-permute-start | bytes 786440 | tf_op jit(solution)/shard_map/ppermute | solution.py:32
  150.2 24.7 %collective-permute-start.16 = (bf16[1024,128]{1,0:T(8,128)(2,1)S(1)}, bf16[1024,128]{1,0:T(8,128)(2,1)S(1)}, u32[]{:S(2)}, u32[]{:S(2)}) collective-permute-start(bf16[1024,128]{1,0:T(8,128)(2,1)S(1)} %copy-done.4), channel_id=1, source_target_pairs={{0,6},{1,7},{2,0},{3,1},{4,2},{5,3},{6,4},{7,5},{8,14},{9,15},{10,... | collective-permute-start | bytes 786440 | tf_op jit(solution)/shard_map/ppermute | solution.py:32
  170.8 16.4 %all-to-all-start.4 = ((bf16[8,128,128]{2,1,0:T(8,128)(2,1)}), bf16[8,128,128]{2,1,0:T(8,128)(2,1)}, u32[]{:S(2)}, u32[]{:S(2)}) async-start(bf16[8,128,128]{2,1,0:T(8,128)(2,1)} %broadcast_in_dim.28), calls=%async_computation.4 | async-start | bytes 524288 | tf_op jit(solution)/shard_map/all_to_all | solution.py:226
  174.9 0.7 copy-start.5
  175.6 0.9 copy-start.6
  179.6 0.7 copy-start.8
  180.2 8.8 %copy-start.9 = (bf16[128,512]{1,0:T(8,128)(2,1)S(1)}, bf16[128,512]{1,0:T(8,128)(2,1)}, u32[]{:S(2)}) copy-start(bf16[128,512]{1,0:T(8,128)(2,1)} %copy-done.8) | copy-start | bytes 393220
  180.2 8.8 %collective-permute-start.17 = (bf16[128,1536]{1,0:T(8,128)(2,1)}, bf16[128,1536]{1,0:T(8,128)(2,1)S(1)}, u32[]{:S(2)}, u32[]{:S(2)}) collective-permute-start(bf16[128,1536]{1,0:T(8,128)(2,1)} %get-tuple-element.33), channel_id=1, source_target_pairs={{0,1},{1,0},{2,3},{3,2},{4,5},{5,4},{6,7},{7,6},{8,9},{9,8},{10,11... | collective-permute-start | bytes 1179656 | tf_op jit(solution)/shard_map/ppermute | solution.py:25

commit v2 on v1

--- a/solution.py
+++ b/solution.py
@@ -125,8 +125,7 @@
 
 def pair_kernel(mine, other, kept, *ahead):
     slab = kept.shape[0]
-    kept[...] = mine[:slab, :].astype(F32) + other[:slab, :].astype(F32)
-    for at, out in enumerate(ahead, 1):
+    for at, out in enumerate((kept, *ahead)):
         here = slice(at * slab, (at + 1) * slab)
         out[...] = (mine[here, :].astype(F32) + other[here, :].astype(F32)).astype(BF16)
 
@@ -249,11 +248,9 @@
         flops=6 * part_rows * slab * width,
     )(block, first, own, second)
     other = swap(theirs)
-    kept, *ahead = call(
-        pair_kernel, [((slab, width), F32)] + [((slab, width), BF16)] * (chips - 1), (0, 2)
-    )(mine, other)
+    kept, *ahead = call(pair_kernel, [((slab, width), BF16)] * chips, (0, 2))(mine, other)
     arrived = [rotate(block, by) for by, block in enumerate(ahead, 1)]
-    agg = (kept + sum(block.astype(F32) for block in arrived)).astype(BF16)
+    agg = sum(block.astype(F32) for block in (kept, *arrived)).astype(BF16)
     core = where[0] % CORES
     mine_cols = packed.reshape(chips, CORES, slab + depth + PAD, out_cols)
     mine_cols = lax.dynamic_index_in_dim(mine_cols, core, 1, keepdims=False)

time: 192 us -> 192 us (level)
  no operation moved by 1% of the time
where the time goes in v2:
time: 192 us; the launch traced here: 190 us
  waiting for transfers between devices  83.2 us (43%)
  starting transfers between devices  82.6 us (43%)
  Pallas kernels  12.5 us (7%)
  local copies, waits for them, and re-layouts  6.51 us (3%)
  other arithmetic  3.88 us (2%)
    all_to_all x4, waiting for transfers between devices, over_row(): return lax.all_to_all(x, 'row', 0, 0, tiled=True, axis_index_groups=groups)  39.2 us
    ppermute x9, waiting for transfers between devices, rotate(): return lax.ppermute(x, 'col', pairs)  36.6 us
    all_to_all x4, starting transfers between devices, over_row(): return lax.all_to_all(x, 'row', 0, 0, tiled=True, axis_index_groups=groups)  27 us
    ppermute x9, starting transfers between devices, rotate(): return lax.ppermute(x, 'col', pairs)  24.3 us
    ppermute x7, starting transfers between devices, swap(): lax.ppermute(x, 'col', [(i, i ^ 1) for i in range(lax.axis_size('col'))])  14 us
    ppermute x2, starting transfers between devices, paired(): return lax.ppermute(x, axis, pairs + [(j, i) for i, j in pairs])  8.56 us
    all_to_all x1, starting transfers between devices, per_device(): packed = lax.all_to_all(packed, 'col', 0, 0, tiled=True)  6.85 us
  transfers between devices with their start and end apart: 24, of which 10 were waited for; matrix products, arithmetic and copies ran while one was open for 2% of the time, Pallas kernels for 3%

profile of v2, /device:TPU:24, one launch (start us, length us, event | category | flops | bytes accessed | tf_op | source)
XLA Modules:
  0.0 190.5 jit_solution(6580271606820535589)
XLA Ops:
  0.6 0.7 convert_rsqrt_fusion
  1.3 1.1 multiply_convert_fusion
  2.4 0.7 collective-permute-start
  3.1 7.9 %collective-permute-start.1 = (bf16[128,1024]{1,0:T(8,128)(2,1)S(1)}, bf16[128,1024]{1,0:T(8,128)(2,1)S(1)}, u32[]{:S(2)}, u32[]{:S(2)}) collective-permute-start(bf16[128,1024]{1,0:T(8,128)(2,1)S(1)} %multiply_convert_fusion), channel_id=1, source_target_pairs={{0,8},{16,24},{32,40},{48,56},{64,72},{80,88},{96,104},{112,120},{... | collective-permute-start | bytes 786440 | tf_op jit(solution)/shard_map/ppermute | solution.py:21
  11.0 0.1 copy.18.scale
  11.8 0.0 copy-start.11
  11.8 0.1 pad_add_fusion.where
  11.9 0.6 copy-done.11
  12.4 0.9 shard_map.104
  13.4 0.0 collective-permute-done.first
  13.4 3.6 %collective-permute-done.1.second = bf16[128,1024]{1,0:T(8,128)(2,1)S(1)} collective-permute-done((bf16[128,1024]{1,0:T(8,128)(2,1)S(1)}, bf16[128,1024]{1,0:T(8,128)(2,1)S(1)}, u32[]{:S(2)}, u32[]{:S(2)}) %collective-permute-start.1) | collective-permute-done | bytes 262176 | tf_op jit(solution)/shard_map/ppermute | solution.py:21
  17.0 1.8 shard_map.105
  18.8 1.9 %collective-permute-start.2 = (bf16[512,1024]{1,0:T(8,128)(2,1)S(1)}, bf16[512,1024]{1,0:T(8,128)(2,1)S(1)}, u32[]{:S(2)}, u32[]{:S(2)}) collective-permute-start(bf16[512,1024]{1,0:T(8,128)(2,1)S(1)} %get-tuple-element.23), channel_id=1, source_target_pairs={{0,1},{1,0},{2,3},{3,2},{4,5},{5,4},{6,7},{7,6},{8,9},{9,8},{10,11... | collective-permute-start | bytes 3145736 | tf_op jit(solution)/shard_map/ppermute | solution.py:25
  20.7 2.6 %collective-permute-done.2.other = bf16[512,1024]{1,0:T(8,128)(2,1)S(1)} collective-permute-done((bf16[512,1024]{1,0:T(8,128)(2,1)S(1)}, bf16[512,1024]{1,0:T(8,128)(2,1)S(1)}, u32[]{:S(2)}, u32[]{:S(2)}) %collective-permute-start.2) | collective-permute-done | bytes 1048608 | tf_op jit(solution)/shard_map/ppermute | solution.py:25
  23.3 0.2 shard_map.106
  23.6 2.1 %collective-permute-start.3 = (bf16[128,1024]{1,0:T(8,128)(2,1)S(1)}, bf16[128,1024]{1,0:T(8,128)(2,1)S(1)}, u32[]{:S(2)}, u32[]{:S(2)}) collective-permute-start(bf16[128,1024]{1,0:T(8,128)(2,1)S(1)} %get-tuple-element.25), channel_id=1, source_target_pairs={{0,2},{1,3},{2,4},{3,5},{4,6},{5,7},{6,0},{7,1},{8,10},{9,11},{10,... | collective-permute-start | bytes 786440 | tf_op jit(solution)/shard_map/ppermute | solution.py:32
  25.7 3.6 %collective-permute-start.4 = (bf16[128,1024]{1,0:T(8,128)(2,1)S(1)}, bf16[128,1024]{1,0:T(8,128)(2,1)S(1)}, u32[]{:S(2)}, u32[]{:S(2)}) collective-permute-start(bf16[128,1024]{1,0:T(8,128)(2,1)S(1)} %get-tuple-element.26), channel_id=1, source_target_pairs={{0,4},{1,5},{2,6},{3,7},{4,0},{5,1},{6,2},{7,3},{8,12},{9,13},{10,... | collective-permute-start | bytes 786440 | tf_op jit(solution)/shard_map/ppermute | solution.py:32
  29.3 0.0 copy-start.10
  29.3 2.4 %collective-permute-start.5 = (bf16[128,1024]{1,0:T(8,128)(2,1)S(1)}, bf16[128,1024]{1,0:T(8,128)(2,1)S(1)}, u32[]{:S(2)}, u32[]{:S(2)}) collective-permute-start(bf16[128,1024]{1,0:T(8,128)(2,1)S(1)} %get-tuple-element.27), channel_id=1, source_target_pairs={{0,6},{1,7},{2,0},{3,1},{4,2},{5,3},{6,4},{7,5},{8,14},{9,15},{10,... | collective-permute-start | bytes 786440 | tf_op jit(solution)/shard_map/ppermute | solution.py:32
  31.7 1.4 shard_map.103
  33.2 6.8 %all-to-all-start = ((bf16[8,272,128]{2,1,0:T(8,128)(2,1)}), bf16[8,272,128]{2,1,0:T(8,128)(2,1)S(1)}, u32[]{:S(2)}, u32[]{:S(2)}) async-start(bf16[8,272,128]{2,1,0:T(8,128)(2,1)} %shard_map.103), calls=%async_computation | async-start | bytes 1114112 | tf_op jit(solution)/shard_map/all_to_all | solution.py:238
  40.0 20.8 %collective-permute-done.4 = bf16[128,1024]{1,0:T(8,128)(2,1)S(1)} collective-permute-done((bf16[128,1024]{1,0:T(8,128)(2,1)S(1)}, bf16[128,1024]{1,0:T(8,128)(2,1)S(1)}, u32[]{:S(2)}, u32[]{:S(2)}) %collective-permute-start.4) | collective-permute-done | bytes 262176 | tf_op jit(solution)/shard_map/ppermute | solution.py:32
  60.8 0.0 collective-permute-done.5
  60.8 0.2 add_convert_fusion.refs_0_.agg
  61.0 1.9 %collective-permute-start.8 = (bf16[128,1024]{1,0:T(8,128)(2,1)S(1)}, bf16[128,1024]{1,0:T(8,128)(2,1)S(1)}, u32[]{:S(2)}, u32[]{:S(2)}) collective-permute-start(bf16[128,1024]{1,0:T(8,128)(2,1)S(1)} %add_convert_fusion.refs_0_.agg), channel_id=1, source_target_pairs={{0,2},{1,3},{2,4},{3,5},{4,6},{5,7},{6,0},{7,1},{8,10},{9,11},{10,... | collective-permute-start | bytes 786440 | tf_op jit(solution)/shard_map/ppermute | solution.py:32
  62.9 2.6 %collective-permute-start.9 = (bf16[128,1024]{1,0:T(8,128)(2,1)S(1)}, bf16[128,1024]{1,0:T(8,128)(2,1)S(1)}, u32[]{:S(2)}, u32[]{:S(2)}) collective-permute-start(bf16[128,1024]{1,0:T(8,128)(2,1)S(1)} %add_convert_fusion.refs_0_.agg), channel_id=1, source_target_pairs={{0,4},{1,5},{2,6},{3,7},{4,0},{5,1},{6,2},{7,3},{8,12},{9,13},{10,... | collective-permute-start | bytes 786440 | tf_op jit(solution)/shard_map/ppermute | solution.py:32
  65.5 3.9 %collective-permute-start.10 = (bf16[128,1024]{1,0:T(8,128)(2,1)S(1)}, bf16[128,1024]{1,0:T(8,128)(2,1)S(1)}, u32[]{:S(2)}, u32[]{:S(2)}) collective-permute-start(bf16[128,1024]{1,0:T(8,128)(2,1)S(1)} %add_convert_fusion.refs_0_.agg), channel_id=1, source_target_pairs={{0,6},{1,7},{2,0},{3,1},{4,2},{5,3},{6,4},{7,5},{8,14},{9,15},{10,... | collective-permute-start | bytes 786440 | tf_op jit(solution)/shard_map/ppermute | solution.py:32
  69.5 1.9 %collective-permute-start.6 = (bf16[128,1024]{1,0:T(8,128)(2,1)S(1)}, bf16[128,1024]{1,0:T(8,128)(2,1)S(1)}, u32[]{:S(2)}, u32[]{:S(2)}) collective-permute-start(bf16[128,1024]{1,0:T(8,128)(2,1)S(1)} %add_convert_fusion.refs_0_.agg), channel_id=1, source_target_pairs={{0,1},{1,0},{2,3},{3,2},{4,5},{5,4},{6,7},{7,6},{8,9},{9,8},{10,11... | collective-permute-start | bytes 786440 | tf_op jit(solution)/shard_map/ppermute | solution.py:25
  71.4 0.9 collective-permute-done.8.refs_1_
  72.3 1.9 %collective-permute-start.11 = (bf16[128,1024]{1,0:T(8,128)(2,1)S(1)}, bf16[128,1024]{1,0:T(8,128)(2,1)S(1)}, u32[]{:S(2)}, u32[]{:S(2)}) collective-permute-start(bf16[128,1024]{1,0:T(8,128)(2,1)S(1)} %collective-permute-done.8.refs_1_), channel_id=1, source_target_pairs={{0,1},{1,0},{2,3},{3,2},{4,5},{5,4},{6,7},{7,6},{8,9},{9,8},{10,11... | collective-permute-start | bytes 786440 | tf_op jit(solution)/shard_map/ppermute | solution.py:25
  74.2 14.9 %collective-permute-done.9.refs_2_ = bf16[128,1024]{1,0:T(8,128)(2,1)S(1)} collective-permute-done((bf16[128,1024]{1,0:T(8,128)(2,1)S(1)}, bf16[128,1024]{1,0:T(8,128)(2,1)S(1)}, u32[]{:S(2)}, u32[]{:S(2)}) %collective-permute-start.9) | collective-permute-done | bytes 262176 | tf_op jit(solution)/shard_map/ppermute | solution.py:32
  89.1 1.9 %collective-permute-start.12 = (bf16[128,1024]{1,0:T(8,128)(2,1)S(1)}, bf16[128,1024]{1,0:T(8,128)(2,1)S(1)}, u32[]{:S(2)}, u32[]{:S(2)}) collective-permute-start(bf16[128,1024]{1,0:T(8,128)(2,1)S(1)} %collective-permute-done.9.refs_2_), channel_id=1, source_target_pairs={{0,1},{1,0},{2,3},{3,2},{4,5},{5,4},{6,7},{7,6},{8,9},{9,8},{10,11... | collective-permute-start | bytes 786440 | tf_op jit(solution)/shard_map/ppermute | solution.py:25
  91.1 0.0 collective-permute-done.10.refs_3_
  91.1 2.4 %collective-permute-start.13 = (bf16[128,1024]{1,0:T(8,128)(2,1)S(1)}, bf16[128,1024]{1,0:T(8,128)(2,1)S(1)}, u32[]{:S(2)}, u32[]{:S(2)}) collective-permute-start(bf16[128,1024]{1,0:T(8,128)(2,1)S(1)} %collective-permute-done.10.refs_3_), channel_id=1, source_target_pairs={{0,1},{1,0},{2,3},{3,2},{4,5},{5,4},{6,7},{7,6},{8,9},{9,8},{10,11... | collective-permute-start | bytes 786440 | tf_op jit(solution)/shard_map/ppermute | solution.py:25
  93.5 0.0 all-to-all-done.packed
  93.5 0.0 collective-permute-done.6.refs_4_.other_agg
  93.5 1.1 collective-permute-done.13.refs_7_
  94.6 3.8 %shard_map.107 = (bf16[1024,128]{1,0:T(8,128)(2,1)S(1)}, bf16[8,128,128]{2,1,0:T(8,128)(2,1)}, f32[128,1]{1,0:T(8,128)S(1)}) custom-call(s32[2]{0:T(128)S(1)} %pad_add_fusion.where, bf16[8,272,128]{2,1,0:T(8,128)(2,1)S(1)} %all-to-all-done.packed, bf16[1024,128]{1,0:T(8,128)(2,1)S(1)} %copy-done, bf16[128,1024]{1,0:T(8,128)(2,1)S(1)} %add_convert_fusion.refs_0_.agg, ...), custom_call_target="tpu_custom_call" | custom-call | flops 536870912 | bytes 2097152 | tf_op jit(solution)/shard_map/pallas_call | solution.py:260
  98.4 0.7 copy-done.3
  99.1 4.7 %all-to-all-start.2 = ((bf16[8,128,128]{2,1,0:T(8,128)(2,1)}), bf16[8,128,128]{2,1,0:T(8,128)(2,1)S(1)}, u32[]{:S(2)}, u32[]{:S(2)}) async-start(bf16[8,128,128]{2,1,0:T(8,128)(2,1)} %get-tuple-element.36), calls=%async_computation.2 | async-start | bytes 524288 | tf_op jit(solution)/shard_map/all_to_all | solution.py:225
  103.8 12.4 %all-to-all-done.2 = bf16[8,128,128]{2,1,0:T(8,128)(2,1)S(1)} async-done(((bf16[8,128,128]{2,1,0:T(8,128)(2,1)}), bf16[8,128,128]{2,1,0:T(8,128)(2,1)S(1)}, u32[]{:S(2)}, u32[]{:S(2)}) %all-to-all-start.2) | async-done | bytes 262176 | tf_op jit(solution)/shard_map/all_to_all | solution.py:225
  116.2 0.1 copy.21
  116.3 0.7 broadcast_in_dim.13
  117.0 14.6 %all-to-all-start.3 = ((bf16[4,128,128]{2,1,0:T(8,128)(2,1)}), bf16[4,128,128]{2,1,0:T(8,128)(2,1)S(1)}, u32[]{:S(2)}, u32[]{:S(2)}) async-start(bf16[4,128,128]{2,1,0:T(8,128)(2,1)} %broadcast_in_dim.13), calls=%async_computation.3 | async-start | bytes 262144 | tf_op jit(solution)/shard_map/all_to_all | solution.py:225
  131.6 5.9 %all-to-all-done.3 = bf16[4,128,128]{2,1,0:T(8,128)(2,1)S(1)} async-done(((bf16[4,128,128]{2,1,0:T(8,128)(2,1)}), bf16[4,128,128]{2,1,0:T(8,128)(2,1)S(1)}, u32[]{:S(2)}, u32[]{:S(2)}) %all-to-all-start.3) | async-done | bytes 131104 | tf_op jit(solution)/shard_map/all_to_all | solution.py:225
  137.6 1.2 broadcast_in_dim.11
  138.8 3.7 %all-to-all-start.1 = ((bf16[8,4,128,128]{3,2,1,0:T(8,128)(2,1)}), bf16[8,4,128,128]{3,2,1,0:T(8,128)(2,1)S(1)}, u32[]{:S(2)}, u32[]{:S(2)}) async-start(bf16[8,4,128,128]{3,2,1,0:T(8,128)(2,1)} %broadcast_in_dim.11), calls=%async_computation.1 | async-start | bytes 2097152 | tf_op jit(solution)/shard_map/all_to_all | solution.py:225
  142.5 1.9 %collective-permute-start.18 = (bf16[128,128]{1,0:T(8,128)(2,1)S(1)}, bf16[128,128]{1,0:T(8,128)(2,1)S(1)}, u32[]{:S(2)}, u32[]{:S(2)}) collective-permute-start(bf16[128,128]{1,0:T(8,128)(2,1)S(1)} %reduce_sum.25), channel_id=1, source_target_pairs={{0,256},{8,264},{16,272},{24,280},{32,288},{40,296},{48,304},{56,3... | collective-permute-start | bytes 98312 | tf_op jit(solution)/shard_map/ppermute | solution.py:278
  144.5 1.9 %collective-permute-start.7 = (bf16[1024,128]{1,0:T(8,128)(2,1)S(1)}, bf16[1024,128]{1,0:T(8,128)(2,1)S(1)}, u32[]{:S(2)}, u32[]{:S(2)}) collective-permute-start(bf16[1024,128]{1,0:T(8,128)(2,1)S(1)} %get-tuple-element.28.middle), channel_id=1, source_target_pairs={{0,1},{1,0},{2,3},{3,2},{4,5},{5,4},{6,7},{7,6},{8,9},{9,8},{10,11... | collective-permute-start | bytes 786440 | tf_op jit(solution)/shard_map/ppermute | solution.py:25
  146.4 1.9 %collective-permute-start.14 = (bf16[1024,128]{1,0:T(8,128)(2,1)S(1)}, bf16[1024,128]{1,0:T(8,128)(2,1)S(1)}, u32[]{:S(2)}, u32[]{:S(2)}) collective-permute-start(bf16[1024,128]{1,0:T(8,128)(2,1)S(1)} %copy-done.4), channel_id=1, source_target_pairs={{0,2},{1,3},{2,4},{3,5},{4,6},{5,7},{6,0},{7,1},{8,10},{9,11},{10,... | collective-permute-start | bytes 786440 | tf_op jit(solution)/shard_map/ppermute | solution.py:32
  148.3 1.9 %collective-permute-start.15 = (bf16[1024,128]{1,0:T(8,128)(2,1)S(1)}, bf16[1024,128]{1,0:T(8,128)(2,1)S(1)}, u32[]{:S(2)}, u32[]{:S(2)}) collective-permute-start(bf16[1024,128]{1,0:T(8,128)(2,1)S(1)} %copy-done.4), channel_id=1, source_target_pairs={{0,4},{1,5},{2,6},{3,7},{4,0},{5,1},{6,2},{7,3},{8,12},{9,13},{10,... | collective-permute-start | bytes 786440 | tf_op jit(solution)/shard_map/ppermute | solution.py:32
  150.3 3.9 %collective-permute-start.16 = (bf16[1024,128]{1,0:T(8,128)(2,1)S(1)}, bf16[1024,128]{1,0:T(8,128)(2,1)S(1)}, u32[]{:S(2)}, u32[]{:S(2)}) collective-permute-start(bf16[1024,128]{1,0:T(8,128)(2,1)S(1)} %copy-done.4), channel_id=1, source_target_pairs={{0,6},{1,7},{2,0},{3,1},{4,2},{5,3},{6,4},{7,5},{8,14},{9,15},{10,... | collective-permute-start | bytes 786440 | tf_op jit(solution)/shard_map/ppermute | solution.py:32
  154.2 15.9 %all-to-all-done.1.weight = bf16[8,4,128,128]{3,2,1,0:T(8,128)(2,1)S(1)} async-done(((bf16[8,4,128,128]{3,2,1,0:T(8,128)(2,1)}), bf16[8,4,128,128]{3,2,1,0:T(8,128)(2,1)S(1)}, u32[]{:S(2)}, u32[]{:S(2)}) %all-to-all-start.1) | async-done | bytes 1048608 | tf_op jit(solution)/shard_map/all_to_all | solution.py:225
  170.1 0.7 broadcast_in_dim.28
  170.9 4.1 %all-to-all-start.4 = ((bf16[8,128,128]{2,1,0:T(8,128)(2,1)}), bf16[8,128,128]{2,1,0:T(8,128)(2,1)}, u32[]{:S(2)}, u32[]{:S(2)}) async-start(bf16[8,128,128]{2,1,0:T(8,128)(2,1)} %broadcast_in_dim.28), calls=%async_computation.4 | async-start | bytes 524288 | tf_op jit(solution)/shard_map/all_to_all | solution.py:225
  175.0 0.0 copy-start.5
  175.0 0.7 copy-done.5
  175.7 0.9 copy-done.6
  176.6 3.0 %shard_map.108 = (bf16[128,512]{1,0:T(8,128)(2,1)S(1)}, f32[128,1024]{1,0:T(8,128)S(1)}, bf16[128,1536]{1,0:T(8,128)(2,1)}) custom-call(s32[2]{0:T(128)S(1)} %pad_add_fusion.where, bf16[8,4,128,128]{3,2,1,0:T(8,128)(2,1)S(1)} %all-to-all-done.1.weight, bf16[128,1024]{1,0:T(8,128)(2,1)S(1)} %add_convert_fusion.refs_0_.agg, ...), custom_call_target="tpu_custom_call" | custom-call | flops 805306368 | bytes 2097152 | tf_op jit(solution)/shard_map/pallas_call | solution.py:284
  179.6 0.7 copy-done.8
  180.3 2.1 %collective-permute-start.17 = (bf16[128,1536]{1,0:T(8,128)(2,1)}, bf16[128,1536]{1,0:T(8,128)(2,1)S(1)}, u32[]{:S(2)}, u32[]{:S(2)}) collective-permute-start(bf16[128,1536]{1,0:T(8,128)(2,1)} %get-tuple-element.33), channel_id=1, source_target_pairs={{0,1},{1,0},{2,3},{3,2},{4,5},{5,4},{6,7},{7,6},{8,9},{9,8},{10,11... | collective-permute-start | bytes 1179656 | tf_op jit(solution)/shard_map/ppermute | solution.py:25
  182.3 4.9 %all-to-all-done.4 = bf16[8,128,128]{2,1,0:T(8,128)(2,1)} async-done(((bf16[8,128,128]{2,1,0:T(8,128)(2,1)}), bf16[8,128,128]{2,1,0:T(8,128)(2,1)}, u32[]{:S(2)}, u32[]{:S(2)}) %all-to-all-start.4) | async-done | bytes 262176 | tf_op jit(solution)/shard_map/all_to_all | solution.py:225
  187.2 1.8 bitcast_convert_fusion
  189.0 1.4 shard_map.109
  (30 shorter events, 0.2 us)
Async XLA Ops:
  1.3 10.6 %copy-start.2 = (bf16[128,1024]{1,0:T(8,128)(2,1)S(1)}, bf16[128,1024]{1,0:T(8,128)(2,1)}, u32[]{:S(2)}) copy-start(bf16[128,1024]{1,0:T(8,128)(2,1)} %feats.1) | copy-start | bytes 786436
  1.3 10.6 %copy-start.7 = (bf16[6,128,128]{2,1,0:T(8,128)(2,1)S(1)}, bf16[6,128,128]{2,1,0:T(8,128)(2,1)}, u32[]{:S(2)}) copy-start(bf16[6,128,128]{2,1,0:T(8,128)(2,1)} %tiles.1) | copy-start | bytes 589828
  2.4 10.9 %collective-permute-start = (bf16[128,1024]{1,0:T(8,128)(2,1)S(1)}, bf16[128,1024]{1,0:T(8,128)(2,1)S(1)}, u32[]{:S(2)}, u32[]{:S(2)}) collective-permute-start(bf16[128,1024]{1,0:T(8,128)(2,1)S(1)} %multiply_convert_fusion), channel_id=1, source_target_pairs={{8,16},{24,32},{40,48},{56,64},{72,80},{88,96},{104,112},{120,128}... | collective-permute-start | bytes 786440 | tf_op jit(solution)/shard_map/ppermute | solution.py:21
  3.1 13.9 %collective-permute-start.1 = (bf16[128,1024]{1,0:T(8,128)(2,1)S(1)}, bf16[128,1024]{1,0:T(8,128)(2,1)S(1)}, u32[]{:S(2)}, u32[]{:S(2)}) collective-permute-start(bf16[128,1024]{1,0:T(8,128)(2,1)S(1)} %multiply_convert_fusion), channel_id=1, source_target_pairs={{0,8},{16,24},{32,40},{48,56},{64,72},{80,88},{96,104},{112,120},{... | collective-permute-start | bytes 786440 | tf_op jit(solution)/shard_map/ppermute | solution.py:21
  11.8 0.7 copy-start.11
  18.8 4.6 %collective-permute-start.2 = (bf16[512,1024]{1,0:T(8,128)(2,1)S(1)}, bf16[512,1024]{1,0:T(8,128)(2,1)S(1)}, u32[]{:S(2)}, u32[]{:S(2)}) collective-permute-start(bf16[512,1024]{1,0:T(8,128)(2,1)S(1)} %get-tuple-element.23), channel_id=1, source_target_pairs={{0,1},{1,0},{2,3},{3,2},{4,5},{5,4},{6,7},{7,6},{8,9},{9,8},{10,11... | collective-permute-start | bytes 3145736 | tf_op jit(solution)/shard_map/ppermute | solution.py:25
  23.3 8.4 %copy-start = (bf16[1024,128]{1,0:T(8,128)(2,1)S(1)}, bf16[1024,128]{1,0:T(8,128)(2,1)}, u32[]{:S(2)}) copy-start(bf16[1024,128]{1,0:T(8,128)(2,1)} %weight.3) | copy-start | bytes 786436
  23.3 8.4 %copy-start.1 = (bf16[128,1024]{1,0:T(8,128)(2,1)S(1)}, bf16[128,1024]{1,0:T(8,128)(2,1)}, u32[]{:S(2)}) copy-start(bf16[128,1024]{1,0:T(8,128)(2,1)} %cot.1) | copy-start | bytes 786436
  23.6 16.4 %collective-permute-start.3 = (bf16[128,1024]{1,0:T(8,128)(2,1)S(1)}, bf16[128,1024]{1,0:T(8,128)(2,1)S(1)}, u32[]{:S(2)}, u32[]{:S(2)}) collective-permute-start(bf16[128,1024]{1,0:T(8,128)(2,1)S(1)} %get-tuple-element.25), channel_id=1, source_target_pairs={{0,2},{1,3},{2,4},{3,5},{4,6},{5,7},{6,0},{7,1},{8,10},{9,11},{10,... | collective-permute-start | bytes 786440 | tf_op jit(solution)/shard_map/ppermute | solution.py:32
  25.7 35.1 %collective-permute-start.4 = (bf16[128,1024]{1,0:T(8,128)(2,1)S(1)}, bf16[128,1024]{1,0:T(8,128)(2,1)S(1)}, u32[]{:S(2)}, u32[]{:S(2)}) collective-permute-start(bf16[128,1024]{1,0:T(8,128)(2,1)S(1)} %get-tuple-element.26), channel_id=1, source_target_pairs={{0,4},{1,5},{2,6},{3,7},{4,0},{5,1},{6,2},{7,3},{8,12},{9,13},{10,... | collective-permute-start | bytes 786440 | tf_op jit(solution)/shard_map/ppermute | solution.py:32
  29.3 2.4 %copy-start.10 = (s32[128]{0:T(128)S(1)}, s32[128]{0:T(128)}, u32[]{:S(2)}) copy-start(s32[128]{0:T(128)} %param.10) | copy-start | bytes 1540
  29.3 31.5 %collective-permute-start.5 = (bf16[128,1024]{1,0:T(8,128)(2,1)S(1)}, bf16[128,1024]{1,0:T(8,128)(2,1)S(1)}, u32[]{:S(2)}, u32[]{:S(2)}) collective-permute-start(bf16[128,1024]{1,0:T(8,128)(2,1)S(1)} %get-tuple-element.27), channel_id=1, source_target_pairs={{0,6},{1,7},{2,0},{3,1},{4,2},{5,3},{6,4},{7,5},{8,14},{9,15},{10,... | collective-permute-start | bytes 786440 | tf_op jit(solution)/shard_map/ppermute | solution.py:32
  33.2 60.3 %all-to-all-start = ((bf16[8,272,128]{2,1,0:T(8,128)(2,1)}), bf16[8,272,128]{2,1,0:T(8,128)(2,1)S(1)}, u32[]{:S(2)}, u32[]{:S(2)}) async-start(bf16[8,272,128]{2,1,0:T(8,128)(2,1)} %shard_map.103), calls=%async_computation | async-start | bytes 1114112 | tf_op jit(solution)/shard_map/all_to_all | solution.py:238
  61.0 11.3 %collective-permute-start.8 = (bf16[128,1024]{1,0:T(8,128)(2,1)S(1)}, bf16[128,1024]{1,0:T(8,128)(2,1)S(1)}, u32[]{:S(2)}, u32[]{:S(2)}) collective-permute-start(bf16[128,1024]{1,0:T(8,128)(2,1)S(1)} %add_convert_fusion.refs_0_.agg), channel_id=1, source_target_pairs={{0,2},{1,3},{2,4},{3,5},{4,6},{5,7},{6,0},{7,1},{8,10},{9,11},{10,... | collective-permute-start | bytes 786440 | tf_op jit(solution)/shard_map/ppermute | solution.py:32
  62.9 26.2 %collective-permute-start.9 = (bf16[128,1024]{1,0:T(8,128)(2,1)S(1)}, bf16[128,1024]{1,0:T(8,128)(2,1)S(1)}, u32[]{:S(2)}, u32[]{:S(2)}) collective-permute-start(bf16[128,1024]{1,0:T(8,128)(2,1)S(1)} %add_convert_fusion.refs_0_.agg), channel_id=1, source_target_pairs={{0,4},{1,5},{2,6},{3,7},{4,0},{5,1},{6,2},{7,3},{8,12},{9,13},{10,... | collective-permute-start | bytes 786440 | tf_op jit(solution)/shard_map/ppermute | solution.py:32
  65.5 25.5 %collective-permute-start.10 = (bf16[128,1024]{1,0:T(8,128)(2,1)S(1)}, bf16[128,1024]{1,0:T(8,128)(2,1)S(1)}, u32[]{:S(2)}, u32[]{:S(2)}) collective-permute-start(bf16[128,1024]{1,0:T(8,128)(2,1)S(1)} %add_convert_fusion.refs_0_.agg), channel_id=1, source_target_pairs={{0,6},{1,7},{2,0},{3,1},{4,2},{5,3},{6,4},{7,5},{8,14},{9,15},{10,... | collective-permute-start | bytes 786440 | tf_op jit(solution)/shard_map/ppermute | solution.py:32
  69.5 24.0 %collective-permute-start.6 = (bf16[128,1024]{1,0:T(8,128)(2,1)S(1)}, bf16[128,1024]{1,0:T(8,128)(2,1)S(1)}, u32[]{:S(2)}, u32[]{:S(2)}) collective-permute-start(bf16[128,1024]{1,0:T(8,128)(2,1)S(1)} %add_convert_fusion.refs_0_.agg), channel_id=1, source_target_pairs={{0,1},{1,0},{2,3},{3,2},{4,5},{5,4},{6,7},{7,6},{8,9},{9,8},{10,11... | collective-permute-start | bytes 786440 | tf_op jit(solution)/shard_map/ppermute | solution.py:25
  72.3 21.2 %collective-permute-start.11 = (bf16[128,1024]{1,0:T(8,128)(2,1)S(1)}, bf16[128,1024]{1,0:T(8,128)(2,1)S(1)}, u32[]{:S(2)}, u32[]{:S(2)}) collective-permute-start(bf16[128,1024]{1,0:T(8,128)(2,1)S(1)} %collective-permute-done.8.refs_1_), channel_id=1, source_target_pairs={{0,1},{1,0},{2,3},{3,2},{4,5},{5,4},{6,7},{7,6},{8,9},{9,8},{10,11... | collective-permute-start | bytes 786440 | tf_op jit(solution)/shard_map/ppermute | solution.py:25
  89.1 4.4 %collective-permute-start.12 = (bf16[128,1024]{1,0:T(8,128)(2,1)S(1)}, bf16[128,1024]{1,0:T(8,128)(2,1)S(1)}, u32[]{:S(2)}, u32[]{:S(2)}) collective-permute-start(bf16[128,1024]{1,0:T(8,128)(2,1)S(1)} %collective-permute-done.9.refs_2_), channel_id=1, source_target_pairs={{0,1},{1,0},{2,3},{3,2},{4,5},{5,4},{6,7},{7,6},{8,9},{9,8},{10,11... | collective-permute-start | bytes 786440 | tf_op jit(solution)/shard_map/ppermute | solution.py:25
  91.1 3.6 %collective-permute-start.13 = (bf16[128,1024]{1,0:T(8,128)(2,1)S(1)}, bf16[128,1024]{1,0:T(8,128)(2,1)S(1)}, u32[]{:S(2)}, u32[]{:S(2)}) collective-permute-start(bf16[128,1024]{1,0:T(8,128)(2,1)S(1)} %collective-permute-done.10.refs_3_), channel_id=1, source_target_pairs={{0,1},{1,0},{2,3},{3,2},{4,5},{5,4},{6,7},{7,6},{8,9},{9,8},{10,11... | collective-permute-start | bytes 786440 | tf_op jit(solution)/shard_map/ppermute | solution.py:25
  98.4 0.7 copy-start.3
  99.1 17.1 %all-to-all-start.2 = ((bf16[8,128,128]{2,1,0:T(8,128)(2,1)}), bf16[8,128,128]{2,1,0:T(8,128)(2,1)S(1)}, u32[]{:S(2)}, u32[]{:S(2)}) async-start(bf16[8,128,128]{2,1,0:T(8,128)(2,1)} %get-tuple-element.36), calls=%async_computation.2 | async-start | bytes 524288 | tf_op jit(solution)/shard_map/all_to_all | solution.py:225
  117.0 20.6 %all-to-all-start.3 = ((bf16[4,128,128]{2,1,0:T(8,128)(2,1)}), bf16[4,128,128]{2,1,0:T(8,128)(2,1)S(1)}, u32[]{:S(2)}, u32[]{:S(2)}) async-start(bf16[4,128,128]{2,1,0:T(8,128)(2,1)} %broadcast_in_dim.13), calls=%async_computation.3 | async-start | bytes 262144 | tf_op jit(solution)/shard_map/all_to_all | solution.py:225
  138.8 7.6 %copy-start.4 = (bf16[1024,128]{1,0:T(8,128)(2,1)S(1)}, bf16[1024,128]{1,0:T(8,128)(2,1)}, u32[]{:S(2)}) copy-start(bf16[1024,128]{1,0:T(8,128)(2,1)} %copy-done.3) | copy-start | bytes 786436
  138.8 31.3 %all-to-all-start.1 = ((bf16[8,4,128,128]{3,2,1,0:T(8,128)(2,1)}), bf16[8,4,128,128]{3,2,1,0:T(8,128)(2,1)S(1)}, u32[]{:S(2)}, u32[]{:S(2)}) async-start(bf16[8,4,128,128]{3,2,1,0:T(8,128)(2,1)} %broadcast_in_dim.11), calls=%async_computation.1 | async-start | bytes 2097152 | tf_op jit(solution)/shard_map/all_to_all | solution.py:225
  142.5 11.7 %collective-permute-start.18 = (bf16[128,128]{1,0:T(8,128)(2,1)S(1)}, bf16[128,128]{1,0:T(8,128)(2,1)S(1)}, u32[]{:S(2)}, u32[]{:S(2)}) collective-permute-start(bf16[128,128]{1,0:T(8,128)(2,1)S(1)} %reduce_sum.25), channel_id=1, source_target_pairs={{0,256},{8,264},{16,272},{24,280},{32,288},{40,296},{48,304},{56,3... | collective-permute-start | bytes 98312 | tf_op jit(solution)/shard_map/ppermute | solution.py:278
  144.5 30.5 %collective-permute-start.7 = (bf16[1024,128]{1,0:T(8,128)(2,1)S(1)}, bf16[1024,128]{1,0:T(8,128)(2,1)S(1)}, u32[]{:S(2)}, u32[]{:S(2)}) collective-permute-start(bf16[1024,128]{1,0:T(8,128)(2,1)S(1)} %get-tuple-element.28.middle), channel_id=1, source_target_pairs={{0,1},{1,0},{2,3},{3,2},{4,5},{5,4},{6,7},{7,6},{8,9},{9,8},{10,11... | collective-permute-start | bytes 786440 | tf_op jit(solution)/shard_map/ppermute | solution.py:25
  146.4 28.5 %collective-permute-start.14 = (bf16[1024,128]{1,0:T(8,128)(2,1)S(1)}, bf16[1024,128]{1,0:T(8,128)(2,1)S(1)}, u32[]{:S(2)}, u32[]{:S(2)}) collective-permute-start(bf16[1024,128]{1,0:T(8,128)(2,1)S(1)} %copy-done.4), channel_id=1, source_target_pairs={{0,2},{1,3},{2,4},{3,5},{4,6},{5,7},{6,0},{7,1},{8,10},{9,11},{10,... | collective-permute-start | bytes 786440 | tf_op jit(solution)/shard_map/ppermute | solution.py:32
  148.3 26.6 %collective-permute-start.15 = (bf16[1024,128]{1,0:T(8,128)(2,1)S(1)}, bf16[1024,128]{1,0:T(8,128)(2,1)S(1)}, u32[]{:S(2)}, u32[]{:S(2)}) collective-permute-start(bf16[1024,128]{1,0:T(8,128)(2,1)S(1)} %copy-done.4), channel_id=1, source_target_pairs={{0,4},{1,5},{2,6},{3,7},{4,0},{5,1},{6,2},{7,3},{8,12},{9,13},{10,... | collective-permute-start | bytes 786440 | tf_op jit(solution)/shard_map/ppermute | solution.py:32
  150.3 24.7 %collective-permute-start.16 = (bf16[1024,128]{1,0:T(8,128)(2,1)S(1)}, bf16[1024,128]{1,0:T(8,128)(2,1)S(1)}, u32[]{:S(2)}, u32[]{:S(2)}) collective-permute-start(bf16[1024,128]{1,0:T(8,128)(2,1)S(1)} %copy-done.4), channel_id=1, source_target_pairs={{0,6},{1,7},{2,0},{3,1},{4,2},{5,3},{6,4},{7,5},{8,14},{9,15},{10,... | collective-permute-start | bytes 786440 | tf_op jit(solution)/shard_map/ppermute | solution.py:32
  170.9 16.4 %all-to-all-start.4 = ((bf16[8,128,128]{2,1,0:T(8,128)(2,1)}), bf16[8,128,128]{2,1,0:T(8,128)(2,1)}, u32[]{:S(2)}, u32[]{:S(2)}) async-start(bf16[8,128,128]{2,1,0:T(8,128)(2,1)} %broadcast_in_dim.28), calls=%async_computation.4 | async-start | bytes 524288 | tf_op jit(solution)/shard_map/all_to_all | solution.py:225
  175.0 0.7 copy-start.5
  175.7 0.9 copy-start.6
  179.6 0.7 copy-start.8
  180.3 8.8 %copy-start.9 = (bf16[128,512]{1,0:T(8,128)(2,1)S(1)}, bf16[128,512]{1,0:T(8,128)(2,1)}, u32[]{:S(2)}) copy-start(bf16[128,512]{1,0:T(8,128)(2,1)} %copy-done.8) | copy-start | bytes 393220
  180.3 8.8 %collective-permute-start.17 = (bf16[128,1536]{1,0:T(8,128)(2,1)}, bf16[128,1536]{1,0:T(8,128)(2,1)S(1)}, u32[]{:S(2)}, u32[]{:S(2)}) collective-permute-start(bf16[128,1536]{1,0:T(8,128)(2,1)} %get-tuple-element.33), channel_id=1, source_target_pairs={{0,1},{1,0},{2,3},{3,2},{4,5},{5,4},{6,7},{7,6},{8,9},{9,8},{10,11... | collective-permute-start | bytes 1179656 | tf_op jit(solution)/shard_map/ppermute | solution.py:25
